TPU v7x, 128 devices: a whole 4x4x4 slice. The times are simulated.
128 devices in a mesh: pipe: 2 (over core), tensor: 2 (over x_lo), dp: 32 (over y, z, x_hi).
Axes of the slice: x: 4 (x_hi: 2, x_lo: 2; x = x_hi * 2 + x_lo), y: 4, z: 4, core: 2. Of those that a mesh axis runs over, the one named last changes fastest.
Arguments:
- section_in: bfloat16 [2, 32, 2, 128, 1024], P('pipe', 'dp', 'tensor'), may hold values from -12 to 12
- lengths: int32 [32, 2], P('dp'), may hold values from 32 to 128, as said below
- qkv_weight: bfloat16 [2, 3, 1024, 1024], P('pipe', None, None, 'tensor'), may hold values from -0.75 to 0.75
- qv_bias: bfloat16 [2, 2, 1024], P('pipe', None, 'tensor'), may hold values from -3 to 3
- out_weight: bfloat16 [2, 1024, 1024], P('pipe', 'tensor'), may hold values from -0.5 to 0.5
- up_weight: bfloat16 [2, 1024, 2048], P('pipe', None, 'tensor'), may hold values from -0.1875 to 0.1875
- up_bias: bfloat16 [2, 2048], P('pipe', 'tensor'), may hold values from -3 to 3
- down_weight: bfloat16 [2, 2048, 1024], P('pipe', 'tensor'), may hold values from -0.125 to 0.125
- norm_gains: float32 [2, 2, 1024], P('pipe'), may hold values from 0.5 to 1.5
- row_biases: float32 [2, 4, 1024], P('pipe'), may hold values from -2 to 2
Outputs:
- section_out: float32 [2, 32, 2, 128, 1024], P('pipe', 'dp', 'tensor')
- qkv_grad: float32 [2, 3, 1024, 1024], P('pipe', None, None, 'tensor')
- qv_bias_grad: float32 [2, 2, 1024], P('pipe', None, 'tensor')
- out_grad: float32 [2, 1024, 1024], P('pipe', 'tensor')
- up_grad: float32 [2, 1024, 2048], P('pipe', None, 'tensor')
- up_bias_grad: float32 [2, 2048], P('pipe', 'tensor')
- down_grad: float32 [2, 2048, 1024], P('pipe', 'tensor')
- gain_grad: float32 [2, 2, 1024], P('pipe')
- bias_grad: float32 [2, 4, 1024], P('pipe')
Inputs may be any that keep to these rules, and one draw needn't show every extreme that they name: `lengths`: some sequence has length exactly 128 and some exactly 32.
All inputs are finite; a program needn't handle non-finite values.
Results may differ from a plain program's by a relative error of at most 0.023.
Values may be sent and summed in bfloat16 or wider, within the bound.
No kernel may reach another device: no remote copies, remote signals or barrier semaphores. Data moves between devices by JAX's collectives and lax.ppermute only.
A program may use at most 128 MiB of HBM per device.

v0:
```python
import jax
import jax.numpy as jnp
from jax import lax
from jax.experimental import pallas as pl
from jax.experimental.pallas import tpu as pltpu
from jax.sharding import Mesh
from jax.sharding import PartitionSpec as P

HEADS = 16
HD = 64
LEN = 128
norm_eps = 1e-05

f32 = jnp.float32
bf16 = jnp.bfloat16

SWAP = ((0, 1), (1, 0))
PAIR_E = ((0, 1), (1, 0), (2, 3), (3, 2))
PAIR_F = ((0, 3), (3, 0), (1, 2), (2, 1))
DP = ("y", "z", "xh")
ROUNDS = (("y", PAIR_E), ("y", PAIR_F), ("z", PAIR_E), ("z", PAIR_F), ("xh", SWAP))


GELU_A = 0.7978845608028654
GELU_B = 0.044715
WIDTH = 1024
HEADS_DEV = HEADS // 2
LOCAL = HEADS_DEV * HD
PAIR = 2 * HD


def matmul(left, right):
    return jnp.dot(left, right, preferred_element_type=f32)


def matmul_nt(left, right):
    return lax.dot_general(left, right, (((1,), (1,)), ((), ())), preferred_element_type=f32)


def matmul_tn(left, right):
    return lax.dot_general(left, right, (((0,), (0,)), ((), ())), preferred_element_type=f32)


def norm_stats(values):
    centred = values - jnp.mean(values, axis=-1, keepdims=True)
    inv_std = lax.rsqrt(jnp.mean(centred * centred, axis=-1, keepdims=True) + norm_eps)
    return centred * inv_std, inv_std


def norm_back(grad_norm, normed, inv_std, gain):
    scaled = grad_norm * gain
    return inv_std * (
        scaled
        - jnp.mean(scaled, axis=-1, keepdims=True)
        - normed * jnp.mean(scaled * normed, axis=-1, keepdims=True)
    )


QV, UP_B, GAIN_A, GAIN_M, SHIFT_A, SHIFT_O, SHIFT_M, SHIFT_D = range(8)


def row(table, index):
    return table[index : index + 1, :]


def table_of(rows):
    zero = jnp.zeros((1, WIDTH), f32)
    return jnp.concatenate([rows.get(index, zero) for index in range(8)], axis=0)


def column_sum(block):
    return jnp.sum(block, axis=0, keepdims=True)


def head_lanes():
    return lax.broadcasted_iota(jnp.int32, (LEN, PAIR), 1) < HD


def attention_rows(rows, table, core, slopes, qkv_w, out_w, outs):
    attn_rows_ref, proj_ref, prob_ref, context_ref, part_ref, sent_ref = outs
    normed, _ = norm_stats(rows.astype(f32))
    attn_rows = (normed * row(table, GAIN_A) + row(table, SHIFT_A)).astype(bf16)
    attn_rows_ref[...] = attn_rows
    for c in range(3):
        block = matmul(attn_rows, qkv_w[c])
        if c == 0:
            block = block + table[QV : QV + 1, :LOCAL]
        if c == 2:
            block = block + table[QV : QV + 1, LOCAL:]
        proj_ref[c] = block.astype(bf16)
    spot_i = lax.broadcasted_iota(jnp.int32, (LEN, LEN), 0)
    spot_j = lax.broadcasted_iota(jnp.int32, (LEN, LEN), 1)
    allowed = (spot_j <= spot_i) & (spot_j < core[1])
    offsets = (spot_i - spot_j).astype(f32)
    first = head_lanes()
    for pair in range(HEADS_DEV // 2):
        lanes = slice(pair * PAIR, (pair + 1) * PAIR)
        query, key, value = (proj_ref[c, :, lanes] for c in range(3))
        found = []
        for side in range(2):
            head = 2 * pair + side
            mine = jnp.where(first if side == 0 else ~first, query, jnp.zeros_like(query))
            scores = matmul_nt(mine, key) * 0.125 - slopes[head] * offsets
            scores = jnp.where(allowed, scores, -jnp.inf)
            top_score = jnp.max(scores, axis=-1, keepdims=True)
            exp_scores = jnp.exp(scores - top_score)
            prob = exp_scores / jnp.sum(exp_scores, axis=-1, keepdims=True)
            prob_ref[head] = prob
            found.append(matmul(prob.astype(bf16), value))
        context_ref[:, lanes] = jnp.where(first, found[0], found[1]).astype(bf16)
    part = matmul(context_ref[...], out_w[...])
    part_ref[...] = part
    sent_ref[...] = part.astype(bf16)


def first_attention(core, slopes, rows, table, qkv_w, out_w, *outs):
    attention_rows(rows[...], table, core, slopes, qkv_w, out_w, outs)


def next_attention(
    core, slopes, resid, part, received, below, table, qkv_w, out_w, out_ref, rows_ref, *outs
):
    layer_out = resid[...] + (part[...] + received[...].astype(f32)) + row(below, SHIFT_D)
    out_ref[...] = layer_out
    rows = layer_out.astype(bf16)
    rows_ref[...] = rows
    attention_rows(rows, table, core, slopes, qkv_w, out_w, outs)


def mlp_forward(
    rows, part, received, table, up_w, down_w, resid_ref, mlp_ref, pre_ref, act_ref, out_ref, sent_ref
):
    resid = (
        rows[...].astype(f32) + (part[...] + received[...].astype(f32)) + row(table, SHIFT_O)
    )
    resid_ref[...] = resid
    normed, _ = norm_stats(resid)
    mlp_rows = (normed * row(table, GAIN_M) + row(table, SHIFT_M)).astype(bf16)
    mlp_ref[...] = mlp_rows
    pre = matmul(mlp_rows, up_w[...]) + row(table, UP_B)
    pre_ref[...] = pre
    act = (0.5 * pre * (1.0 + jnp.tanh(GELU_A * (pre + GELU_B * pre * pre * pre)))).astype(bf16)
    act_ref[...] = act
    out = matmul(act, down_w[...])
    out_ref[...] = out
    sent_ref[...] = out.astype(bf16)


def last_output(resid, part, received, table, out_ref):
    out_ref[...] = resid[...] + (part[...] + received[...].astype(f32)) + row(table, SHIFT_D)


def halves(core, block):
    half = block.shape[1] // 2
    low, high = block[:, :half], block[:, half:]
    own = core[0] == 0
    return jnp.where(own, low, high), jnp.where(own, high, low)


def mlp_back_body(core, grad, pre_in, act, mlp_rows, up_w, down_w, outs):
    pre_half_ref, part_ref, sent_ref, cross_ref, sums_ref = outs
    grad_act = matmul_nt(grad, down_w[...])
    pre = pre_in[...]
    tanh = jnp.tanh(GELU_A * (pre + GELU_B * pre * pre * pre))
    slope = 0.5 * (1.0 + tanh) + 0.5 * pre * (1.0 - tanh * tanh) * (
        GELU_A * (1.0 + 3.0 * GELU_B * pre * pre)
    )
    grad_pre = grad_act * slope
    pre_half = grad_pre.astype(bf16)
    pre_half_ref[...] = pre_half
    part = matmul_nt(pre_half, up_w[...])
    part_ref[...] = part
    sent_ref[...] = part.astype(bf16)
    cross_ref[:, :512] = halves(core, act[...])[1]
    cross_ref[:, 512:1536] = grad
    cross_ref[:, 1536:2048] = halves(core, mlp_rows[...])[1]
    cross_ref[:, 2048:] = pre_half
    return column_sum(grad_pre)


def mlp_backward(core, grad, pre, act, mlp_rows, up_w, down_w, *outs):
    total = mlp_back_body(core, grad[...], pre, act, mlp_rows, up_w, down_w, outs)
    outs[4][...] = table_of({UP_B: total})


def input_grad(grad_resid, part, received, rows, table):
    grad_attn = part[...] + received[...].astype(f32)
    normed, inv_std = norm_stats(rows[...].astype(f32))
    grad_in = grad_resid[...] + norm_back(grad_attn, normed, inv_std, row(table, GAIN_A))
    sums = {GAIN_A: column_sum(grad_attn * normed), SHIFT_A: column_sum(grad_attn)}
    return grad_in, sums


def mlp_backward_below(
    core, grad_resid, da_part, da_received, above_rows, above_table,
    pre, act, mlp_rows, up_w, down_w, grad_ref, above_ref, *outs,
):
    grad_in, sums = input_grad(grad_resid, da_part, da_received, above_rows, above_table)
    above_ref[...] = table_of(sums)
    grad = grad_in.astype(bf16)
    grad_ref[...] = grad
    total = mlp_back_body(core, grad, pre, act, mlp_rows, up_w, down_w, outs)
    outs[4][...] = table_of({UP_B: total})


def last_input_grad(grad_resid, part, received, rows, table, grad_ref, sums_ref):
    grad_in, sums = input_grad(grad_resid, part, received, rows, table)
    grad_ref[...] = grad_in
    sums_ref[...] = table_of(sums)


def attention_backward(
    core, grad_out, dc_part, dc_received, resid, table, out_w, qkv_w, proj, prob_in, context, attn_rows,
    grad_ref, resid_half_ref, proj_grad_ref, part_ref, sent_ref, cross_ref, sums_ref,
):
    grad_mlp = dc_part[...] + dc_received[...].astype(f32)
    normed, inv_std = norm_stats(resid[...])
    wide_out = grad_out[...].astype(f32)
    grad_resid = wide_out + norm_back(grad_mlp, normed, inv_std, row(table, GAIN_M))
    grad_ref[...] = grad_resid
    resid_half = grad_resid.astype(bf16)
    resid_half_ref[...] = resid_half
    grad_context = matmul_nt(resid_half, out_w[...]).astype(bf16)
    first = head_lanes()
    query_sums = []
    value_sums = []
    for pair in range(HEADS_DEV // 2):
        lanes = slice(pair * PAIR, (pair + 1) * PAIR)
        query, key, value = (proj[c, :, lanes] for c in range(3))
        context_grad = grad_context[:, lanes]
        query_g, key_g, value_g = [], [], []
        for side in range(2):
            mask = first if side == 0 else ~first
            prob = prob_in[2 * pair + side]
            mine = jnp.where(mask, context_grad, jnp.zeros_like(context_grad))
            grad_prob = matmul_nt(mine, value)
            value_g.append(matmul_tn(prob.astype(bf16), context_grad))
            delta = jnp.sum(prob * grad_prob, axis=-1, keepdims=True)
            grad_scores = (prob * (grad_prob - delta) * 0.125).astype(bf16)
            query_g.append(matmul(grad_scores, key))
            key_g.append(matmul_tn(grad_scores, query))
        query_g, key_g, value_g = (
            jnp.where(first, low, high) for low, high in (query_g, key_g, value_g)
        )
        query_sums.append(column_sum(query_g))
        value_sums.append(column_sum(value_g))
        proj_grad_ref[0, :, lanes] = query_g.astype(bf16)
        proj_grad_ref[1, :, lanes] = key_g.astype(bf16)
        proj_grad_ref[2, :, lanes] = value_g.astype(bf16)
    part = matmul_nt(proj_grad_ref[0], qkv_w[0])
    part = part + matmul_nt(proj_grad_ref[1], qkv_w[1])
    part = part + matmul_nt(proj_grad_ref[2], qkv_w[2])
    part_ref[...] = part
    sent_ref[...] = part.astype(bf16)
    cross_ref[:, :512] = context[...]
    cross_ref[:, 512:1024] = halves(core, resid_half)[1]
    cross_ref[:, 1024:1536] = halves(core, attn_rows[...])[1]
    for c in range(3):
        cross_ref[:, 1536 + c * LOCAL : 1536 + (c + 1) * LOCAL] = proj_grad_ref[c]
    sums_ref[...] = table_of(
        {
            QV: jnp.concatenate(query_sums + value_sums, axis=1),
            GAIN_M: column_sum(grad_mlp * normed),
            SHIFT_O: column_sum(grad_resid),
            SHIFT_M: column_sum(grad_mlp),
            SHIFT_D: column_sum(wide_out),
        }
    )


def stacked(own, far):
    return jnp.concatenate([own, far], axis=0)


def mlp_weight_grads(core, act, grad, mlp_rows, pre_half, crossed, out_ref):
    left = stacked(halves(core, act[...])[0], crossed[:, :512])
    right = stacked(grad[...], crossed[:, 512:1536])
    out_ref[:512, :] = matmul_tn(left, right).astype(bf16)
    left = stacked(halves(core, mlp_rows[...])[0], crossed[:, 1536:2048])
    right = stacked(pre_half[...], crossed[:, 2048:])
    out_ref[512:, :] = matmul_tn(left, right).astype(bf16)


def attention_weight_grads(core, context, resid_half, attn_rows, proj_grad, crossed, out_ref):
    left = stacked(halves(core, attn_rows[...])[0], crossed[:, 1024:1536])
    for c in range(3):
        far = crossed[:, 1536 + c * LOCAL : 1536 + (c + 1) * LOCAL]
        out_ref[c * 512 : (c + 1) * 512, :] = matmul_tn(left, stacked(proj_grad[c], far)).astype(bf16)
    left = stacked(context[...], crossed[:, :512])
    right = stacked(halves(core, resid_half[...])[0], crossed[:, 512:1024])
    out_ref[1536:, :] = matmul_tn(left, right).astype(bf16)


def device_kernel(body, name, scalars, shapes):
    smem = pl.BlockSpec(memory_space=pltpu.SMEM)
    vmem = pl.BlockSpec(memory_space=pltpu.VMEM)

    def call(*operands):
        return pl.pallas_call(
            body,
            name=name,
            in_specs=[smem] * scalars + [vmem] * (len(operands) - scalars),
            out_specs=[vmem] * len(shapes),
            out_shape=[jax.ShapeDtypeStruct(shape, dtype) for shape, dtype in shapes],
            compiler_params=pltpu.CompilerParams(vmem_limit_bytes=48 * 1024 * 1024),
        )(*operands)

    return call


ROWS = (LEN, WIDTH)
TABLE = ((8, WIDTH), f32)
ATTENTION_OUT = (
    (ROWS, bf16),
    ((3, LEN, LOCAL), bf16),
    ((HEADS_DEV, LEN, LEN), f32),
    ((LEN, LOCAL), bf16),
    (ROWS, f32),
    (ROWS, bf16),
)
MLP_BACK_OUT = ((ROWS, bf16), (ROWS, f32), (ROWS, bf16), ((LEN, 3072), bf16), TABLE)
FIRST_ATTENTION = device_kernel(first_attention, "first_attention", 2, ATTENTION_OUT)
NEXT_ATTENTION = device_kernel(
    next_attention, "next_attention", 2, ((ROWS, f32), (ROWS, bf16)) + ATTENTION_OUT
)
MLP_FORWARD = device_kernel(
    mlp_forward,
    "mlp_forward",
    0,
    ((ROWS, f32), (ROWS, bf16), (ROWS, f32), (ROWS, bf16), (ROWS, f32), (ROWS, bf16)),
)
LAST_OUTPUT = device_kernel(last_output, "last_output", 0, ((ROWS, f32),))
MLP_BACKWARD = device_kernel(mlp_backward, "mlp_backward", 1, MLP_BACK_OUT)
MLP_BACKWARD_BELOW = device_kernel(
    mlp_backward_below, "mlp_backward_below", 1, ((ROWS, bf16), TABLE) + MLP_BACK_OUT
)
ATTENTION_BACKWARD = device_kernel(
    attention_backward,
    "attention_backward",
    1,
    (
        (ROWS, f32),
        (ROWS, bf16),
        ((3, LEN, LOCAL), bf16),
        (ROWS, f32),
        (ROWS, bf16),
        ((LEN, 3072), bf16),
        TABLE,
    ),
)
LAST_INPUT_GRAD = device_kernel(last_input_grad, "last_input_grad", 0, ((ROWS, f32), TABLE))
MLP_WEIGHT_GRADS = device_kernel(mlp_weight_grads, "mlp_weight_grads", 1, (((1024, 1024), bf16),))
ATTENTION_WEIGHT_GRADS = device_kernel(
    attention_weight_grads, "attention_weight_grads", 1, (((2048, 512), bf16),)
)


def reduced(packed):
    ranks = lax.axis_size(DP)
    rows, columns = packed.shape
    pieces = packed.reshape(ranks, rows // ranks, columns)
    pieces = lax.all_to_all(pieces, DP, split_axis=0, concat_axis=0, tiled=True)
    total = jnp.sum(pieces.astype(f32), axis=0).astype(bf16)
    spread = jnp.broadcast_to(total[None], (ranks,) + total.shape)
    return lax.all_to_all(spread, DP, split_axis=0, concat_axis=0, tiled=True)


def local(
    section_in,
    lengths,
    qkv_weight,
    qv_bias,
    out_weight,
    up_weight,
    up_bias,
    down_weight,
    norm_gains,
    row_biases,
):
    core = lax.axis_index("pipe")
    tensor_index = lax.axis_index("tensor")
    place = core * 2 + tensor_index
    both = ("pipe", "tensor")

    own_rows = section_in[0, 0, 0]
    near = lax.ppermute(own_rows, both, ((0, 1), (1, 2)))
    far = lax.ppermute(own_rows, both, ((1, 3),))
    layer_in = jnp.where(place == 0, own_rows, jnp.where(place == 3, far, near))

    table = jnp.concatenate(
        [
            qv_bias[0].astype(f32).reshape(1, WIDTH),
            up_bias[0].astype(f32).reshape(1, WIDTH),
            norm_gains[0],
            row_biases[0],
        ]
    )
    owned = (qkv_weight[0], out_weight[0], up_weight[0], down_weight[0], table)
    other = tuple(lax.ppermute(array, "pipe", SWAP) for array in owned)
    layers = tuple(
        tuple(jnp.where(core == layer, mine, theirs) for mine, theirs in zip(owned, other))
        for layer in range(2)
    )
    cot_near = lax.ppermute(own_rows, both, ((2, 0), (3, 2)))
    cot_far = lax.ppermute(own_rows, both, ((2, 1),))
    cotangent = jnp.where(place == 3, own_rows, jnp.where(place == 1, cot_far, cot_near))

    seq_length = jnp.where(core == 0, lengths[0, 0], lengths[0, 1])
    core_length = jnp.stack([core, seq_length]).astype(jnp.int32)
    head_ids = tensor_index * HEADS_DEV + jnp.arange(HEADS_DEV) + 1
    slopes = 2.0 ** (-8.0 * head_ids.astype(f32) / HEADS)

    def swapped(sent):
        return lax.ppermute(sent, "tensor", SWAP)

    def crossed(sent):
        return lax.ppermute(sent, "pipe", SWAP)

    qkv_0, out_0, up_0, down_0, table_0 = layers[0]
    qkv_1, out_1, up_1, down_1, table_1 = layers[1]

    rows_0 = layer_in
    attn_0, proj_0, prob_0, context_0, part, sent = FIRST_ATTENTION(
        core_length, slopes, rows_0, table_0, qkv_0, out_0
    )
    resid_0, mlp_0, pre_0, act_0, part, sent = MLP_FORWARD(
        rows_0, part, swapped(sent), table_0, up_0, down_0
    )
    _, rows_1, attn_1, proj_1, prob_1, context_1, part, sent = NEXT_ATTENTION(
        core_length, slopes, resid_0, part, swapped(sent), table_0, table_1, qkv_1, out_1
    )
    resid_1, mlp_1, pre_1, act_1, top_part, top_sent = MLP_FORWARD(
        rows_1, part, swapped(sent), table_1, up_1, down_1
    )
    (out_one,) = LAST_OUTPUT(resid_1, top_part, swapped(top_sent), table_1)

    pre_half_1, part, sent, cross_mlp, sums_mlp_1 = MLP_BACKWARD(
        core_length, cotangent, pre_1, act_1, mlp_1, up_1, down_1
    )
    (early_1,) = MLP_WEIGHT_GRADS(
        core_length, act_1, cotangent, mlp_1, pre_half_1, crossed(cross_mlp)
    )
    grad_1, resid_half_1, proj_grad_1, part, sent, cross_attn, sums_attn_1 = ATTENTION_BACKWARD(
        core_length, cotangent, part, swapped(sent), resid_1, table_1, out_1, qkv_1,
        proj_1, prob_1, context_1, attn_1,
    )
    (late_1,) = ATTENTION_WEIGHT_GRADS(
        core_length, context_1, resid_half_1, attn_1, proj_grad_1, crossed(cross_attn)
    )
    grad_half, sums_in_1, pre_half_0, part, sent, cross_mlp, sums_mlp_0 = MLP_BACKWARD_BELOW(
        core_length, grad_1, part, swapped(sent), rows_1, table_1,
        pre_0, act_0, mlp_0, up_0, down_0,
    )
    (early_0,) = MLP_WEIGHT_GRADS(
        core_length, act_0, grad_half, mlp_0, pre_half_0, crossed(cross_mlp)
    )
    grad_0, resid_half_0, proj_grad_0, part, sent, cross_attn, sums_attn_0 = ATTENTION_BACKWARD(
        core_length, grad_half, part, swapped(sent), resid_0, table_0, out_0, qkv_0,
        proj_0, prob_0, context_0, attn_0,
    )
    (late_0,) = ATTENTION_WEIGHT_GRADS(
        core_length, context_0, resid_half_0, attn_0, proj_grad_0, crossed(cross_attn)
    )
    grad_zero, sums_in_0 = LAST_INPUT_GRAD(grad_0, part, swapped(sent), rows_0, table_0)

    def weights_of(layer, early, late):
        def both_halves(mine):
            theirs = lax.ppermute(mine, "pipe", ((1 - layer, layer),))
            return (mine, theirs) if layer == 0 else (theirs, mine)

        early = both_halves(reduced(early).reshape(2, 512, 1024))
        late = both_halves(reduced(late).reshape(4, 512, 512))
        return (
            jnp.concatenate([half[:3] for half in late], axis=1),
            jnp.concatenate([half[3] for half in late], axis=1),
            jnp.concatenate([half[1] for half in early], axis=0),
            jnp.concatenate([half[0] for half in early], axis=0),
        )

    weights_one = weights_of(1, early_1, late_1)
    weights_zero = weights_of(0, early_0, late_0)
    vectors_one = sums_in_1 + sums_mlp_1 + sums_attn_1
    vectors_zero = sums_in_0 + sums_mlp_0 + sums_attn_0

    first = core == 0
    vectors = jnp.where(first, vectors_zero, vectors_one) + crossed(
        jnp.where(first, vectors_one, vectors_zero)
    )
    for axis, pairs in ROUNDS:
        vectors = vectors + lax.ppermute(vectors, axis, pairs)
    shared = vectors[2:]
    shared = 0.5 * (shared + swapped(shared))

    crossing = lax.ppermute(jnp.where(first, out_one, grad_zero), both, ((0, 2), (3, 1)))
    kept_rows = jnp.where(first, grad_zero, out_one)
    section_out = jnp.where(core == tensor_index, kept_rows, crossing)
    qkv_g, out_g, up_g, down_g = (
        jnp.where(first, zero, one).astype(f32) for zero, one in zip(weights_zero, weights_one)
    )
    return (
        section_out[None, None, None],
        qkv_g[None],
        vectors[0].reshape(1, 2, 512),
        out_g[None],
        up_g[None],
        vectors[1][None],
        down_g[None],
        shared[:2][None],
        shared[2:][None],
    )


def solution(mesh):
    fine = Mesh(mesh.devices.reshape(2, 2, 4, 4, 2), ("pipe", "tensor", "y", "z", "xh"))
    dp = ("y", "z", "xh")
    in_specs = (
        P("pipe", dp, "tensor", None, None),
        P(dp, None),
        P("pipe", None, None, "tensor"),
        P("pipe", None, "tensor"),
        P("pipe", "tensor", None),
        P("pipe", None, "tensor"),
        P("pipe", "tensor"),
        P("pipe", "tensor", None),
        P("pipe", None, None),
        P("pipe", None, None),
    )
    out_specs = (
        P("pipe", dp, "tensor", None, None),
        P("pipe", None, None, "tensor"),
        P("pipe", None, "tensor"),
        P("pipe", "tensor", None),
        P("pipe", None, "tensor"),
        P("pipe", "tensor"),
        P("pipe", "tensor", None),
        P("pipe", None, None),
        P("pipe", None, None),
    )
    return jax.shard_map(local, mesh=fine, in_specs=in_specs, out_specs=out_specs, check_vma=False)
```

profile of v0, /device:TPU:0, one launch (start us, length us, event | category | flops | bytes accessed | tf_op | source)
XLA Modules:
  0.0 487.3 jit_solution(7494421465512751006)
XLA Ops:
  5.3 3.6 collective-permute-start.4
  14.8 3.9 collective-permute-start.3
  28.8 5.1 %broadcast_select_fusion = (bf16[3,1024,512]{2,1,0:T(8,128)(2,1)}, bf16[3,1024,512]{2,1,0:T(8,128)(2,1)}) fusion(bf16[3,1024,512]{2,1,0:T(8,128)(2,1)} %collective-permute-done.5, pred[]{:T(512)S(6)} %eq.34, bf16[1,3,1024,512]{3,2,1,0:T(8,128)(2,1)S(1)} %copy-done.43, pred[]{:T(512)S(6)} %eq.13), kind=kLoop, calls=%fused_computation.2 | loop fusion | flops 3145728 | bytes 12582914 | tf_op jit(solution)/shard_map/jit(_where)/select_n | solution.py:401
  33.9 5.4 %first_attention.1 = (bf16[128,1024]{1,0:T(8,128)(2,1)S(1)}, bf16[3,128,512]{2,1,0:T(8,128)(2,1)S(1)}, f32[8,128,128]{2,1,0:T(8,128)S(1)}, bf16[128,512]{1,0:T(8...) custom-call(s32[2]{0:T(128)S(1)} %pad_add_fusion.core, f32[8]{0:T(128)S(1)} %multiply_power_fusion.slopes, ...), custom_call_target="tpu_custom_call" | custom-call | tf_op jit(solution)/shard_map/first_attention/pallas_call | solution.py:299
  41.8 3.9 broadcast_select_fusion.2
  51.6 6.8 %collective-permute-done.10.received = bf16[128,1024]{1,0:T(8,128)(2,1)S(1)} collective-permute-done((bf16[128,1024]{1,0:T(8,128)(2,1)S(1)}, bf16[128,1024]{1,0:T(8,128)(2,1)S(1)}, u32[]{:S(2)}, u32[]{:S(2)}) %collective-permute-start.10) | collective-permute-done | bytes 262176 | tf_op jit(solution)/shard_map/ppermute | solution.py:414
  58.4 5.3 %next_attention.1 = (f32[128,1024]{1,0:T(8,128)}, bf16[128,1024]{1,0:T(8,128)(2,1)S(1)}, bf16[128,1024]{1,0:T(8,128)(2,1)S(1)}, bf16[3,128,512]{2,1,0:T(8,128)(2...) custom-call(s32[2]{0:T(128)S(1)} %pad_add_fusion.core, ...), custom_call_target="tpu_custom_call" | custom-call | tf_op jit(solution)/shard_map/next_attention/pallas_call | solution.py:299
  65.4 6.1 %collective-permute-done.11.received = bf16[128,1024]{1,0:T(8,128)(2,1)S(1)} collective-permute-done((bf16[128,1024]{1,0:T(8,128)(2,1)S(1)}, bf16[128,1024]{1,0:T(8,128)(2,1)S(1)}, u32[]{:S(2)}, u32[]{:S(2)}) %collective-permute-start.11) | collective-permute-done | bytes 262176 | tf_op jit(solution)/shard_map/ppermute | solution.py:414
  84.7 10.8 %all-to-all-start.6 = ((bf16[32,32,1024]{2,1,0:T(8,128)(2,1)}), bf16[32,32,1024]{2,1,0:T(8,128)(2,1)}, u32[]{:S(2)}, u32[]{:S(2)}) async-start(bf16[32,32,1024]{2,1,0:T(8,128)(2,1)} %bitcast.25), calls=%async_computation.6 | async-start | bytes 4194304 | tf_op jit(solution)/shard_map/all_to_all | solution.py:362
  95.6 28.2 %collective-permute-done.12.dc_received = bf16[128,1024]{1,0:T(8,128)(2,1)S(1)} collective-permute-done((bf16[128,1024]{1,0:T(8,128)(2,1)S(1)}, bf16[128,1024]{1,0:T(8,128)(2,1)S(1)}, u32[]{:S(2)}, u32[]{:S(2)}) %collective-permute-start.12) | collective-permute-done | bytes 262176 | tf_op jit(solution)/shard_map/ppermute | solution.py:414
  125.8 6.3 %attention_backward.2 = (f32[128,1024]{1,0:T(8,128)S(1)}, bf16[128,1024]{1,0:T(8,128)(2,1)S(1)}, bf16[3,128,512]{2,1,0:T(8,128)(2,1)S(1)}, f32[128,1024]{1,0:T(8...) custom-call(s32[2]{0:T(128)S(1)} %pad_add_fusion.core, ...), custom_call_target="tpu_custom_call" | custom-call | tf_op jit(solution)/shard_map/attention_backward/pallas_call | solution.py:299
  138.6 14.6 %all-to-all-start.2 = ((bf16[32,64,512]{2,1,0:T(8,128)(2,1)}), bf16[32,64,512]{2,1,0:T(8,128)(2,1)}, u32[]{:S(2)}, u32[]{:S(2)}) async-start(bf16[32,64,512]{2,1,0:T(8,128)(2,1)} %bitcast.16), calls=%async_computation.2 | async-start | bytes 4194304 | tf_op jit(solution)/shard_map/all_to_all | solution.py:362
  153.3 28.2 %collective-permute-done.13.da_received = bf16[128,1024]{1,0:T(8,128)(2,1)S(1)} collective-permute-done((bf16[128,1024]{1,0:T(8,128)(2,1)S(1)}, bf16[128,1024]{1,0:T(8,128)(2,1)S(1)}, u32[]{:S(2)}, u32[]{:S(2)}) %collective-permute-start.13) | collective-permute-done | bytes 262176 | tf_op jit(solution)/shard_map/ppermute | solution.py:414
  183.6 4.3 mlp_backward_below.1
  193.6 13.9 %all-to-all-start.4 = ((bf16[32,32,1024]{2,1,0:T(8,128)(2,1)}), bf16[32,32,1024]{2,1,0:T(8,128)(2,1)}, u32[]{:S(2)}, u32[]{:S(2)}) async-start(bf16[32,32,1024]{2,1,0:T(8,128)(2,1)} %bitcast.22), calls=%async_computation.4 | async-start | bytes 4194304 | tf_op jit(solution)/shard_map/all_to_all | solution.py:362
  207.6 28.2 %collective-permute-done.14.dc_received = bf16[128,1024]{1,0:T(8,128)(2,1)S(1)} collective-permute-done((bf16[128,1024]{1,0:T(8,128)(2,1)S(1)}, bf16[128,1024]{1,0:T(8,128)(2,1)S(1)}, u32[]{:S(2)}, u32[]{:S(2)}) %collective-permute-start.14) | collective-permute-done | bytes 262176 | tf_op jit(solution)/shard_map/ppermute | solution.py:414
  236.8 7.0 %attention_backward.3 = (f32[128,1024]{1,0:T(8,128)S(1)}, bf16[128,1024]{1,0:T(8,128)(2,1)S(1)}, bf16[3,128,512]{2,1,0:T(8,128)(2,1)S(1)}, f32[128,1024]{1,0:T(8...) custom-call(s32[2]{0:T(128)S(1)} %pad_add_fusion.core, ...), custom_call_target="tpu_custom_call" | custom-call | tf_op jit(solution)/shard_map/attention_backward/pallas_call | solution.py:299
  250.3 14.0 %all-to-all-start = ((bf16[32,64,512]{2,1,0:T(8,128)(2,1)}), bf16[32,64,512]{2,1,0:T(8,128)(2,1)}, u32[]{:S(2)}, u32[]{:S(2)}) async-start(bf16[32,64,512]{2,1,0:T(8,128)(2,1)} %bitcast.12), calls=%async_computation | async-start | bytes 4194304 | tf_op jit(solution)/shard_map/all_to_all | solution.py:362
  266.3 29.9 %all-to-all-done = bf16[32,64,512]{2,1,0:T(8,128)(2,1)} async-done(((bf16[32,64,512]{2,1,0:T(8,128)(2,1)}), bf16[32,64,512]{2,1,0:T(8,128)(2,1)}, u32[]{:S(2)}, u32[]{:S(2)}) %all-to-all-start) | async-done | bytes 2097184 | tf_op jit(solution)/shard_map/all_to_all | solution.py:362
  297.8 4.0 all-to-all-start.7
  303.7 28.0 %all-to-all-done.7 = bf16[32,32,1024]{2,1,0:T(8,128)(2,1)S(1)} async-done(((bf16[32,32,1024]{2,1,0:T(8,128)(2,1)}), bf16[32,32,1024]{2,1,0:T(8,128)(2,1)S(1)}, u32[]{:S(2)}, u32[]{:S(2)}) %all-to-all-start.7) | async-done | bytes 2097184 | tf_op jit(solution)/shard_map/all_to_all | solution.py:365
  333.4 4.8 all-to-all-start.3
  340.2 26.8 %all-to-all-done.3 = bf16[32,64,512]{2,1,0:T(8,128)(2,1)} async-done(((bf16[32,64,512]{2,1,0:T(8,128)(2,1)}), bf16[32,64,512]{2,1,0:T(8,128)(2,1)}, u32[]{:S(2)}, u32[]{:S(2)}) %all-to-all-start.3) | async-done | bytes 2097184 | tf_op jit(solution)/shard_map/all_to_all | solution.py:365
  368.6 4.8 all-to-all-start.5
  373.3 4.4 collective-permute-start.15
  379.7 24.3 %all-to-all-done.5 = bf16[32,32,1024]{2,1,0:T(8,128)(2,1)} async-done(((bf16[32,32,1024]{2,1,0:T(8,128)(2,1)}), bf16[32,32,1024]{2,1,0:T(8,128)(2,1)}, u32[]{:S(2)}, u32[]{:S(2)}) %all-to-all-start.5) | async-done | bytes 2097184 | tf_op jit(solution)/shard_map/all_to_all | solution.py:365
  405.6 4.9 %all-to-all-start.1 = ((bf16[32,64,512]{2,1,0:T(8,128)(2,1)}), bf16[32,64,512]{2,1,0:T(8,128)(2,1)}, u32[]{:S(2)}, u32[]{:S(2)}) async-start(bf16[32,64,512]{2,1,0:T(8,128)(2,1)} %broadcast_in_dim.15), calls=%async_computation.1 | async-start | bytes 4194304 | tf_op jit(solution)/shard_map/all_to_all | solution.py:365
  411.2 5.1 %collective-permute-start.16 = (bf16[128,1024]{1,0:T(8,128)(2,1)}, bf16[128,1024]{1,0:T(8,128)(2,1)S(1)}, u32[]{:S(2)}, u32[]{:S(2)}) collective-permute-start(bf16[128,1024]{1,0:T(8,128)(2,1)} %copy-done.41), channel_id=1, source_target_pairs={{0,32},{32,0},{1,33},{33,1},{2,34},{34,2},{3,35},{35,3},{4,36},{36... | collective-permute-start | bytes 786440 | tf_op jit(solution)/shard_map/ppermute | solution.py:414
  418.0 12.8 %collective-permute-done.23 = f32[8,1024]{1,0:T(8,128)S(1)} collective-permute-done((f32[8,1024]{1,0:T(8,128)S(1)}, f32[8,1024]{1,0:T(8,128)S(1)}, u32[]{:S(2)}, u32[]{:S(2)}) %collective-permute-start.23) | collective-permute-done | bytes 32800 | tf_op jit(solution)/shard_map/ppermute | solution.py:490
  432.0 3.9 collective-permute-done.24
  452.3 4.9 %collective-permute-start.32 = (f32[6,1024]{1,0:T(8,128)S(1)}, f32[6,1024]{1,0:T(8,128)S(1)}, u32[]{:S(2)}, u32[]{:S(2)}) collective-permute-start(f32[6,1024]{1,0:T(8,128)S(1)} %slice.118), channel_id=1, source_target_pairs={{0,32},{32,0},{1,33},{33,1},{2,34},{34,2},{3,35},{35,3},{4,36},{36... | collective-permute-start | bytes 73736 | tf_op jit(solution)/shard_map/ppermute | solution.py:414
  478.0 4.4 fusion.1
  (209 shorter events, 126.0 us)
Async XLA Ops:
  0.7 27.5 %collective-permute-start.5 = (bf16[3,1024,512]{2,1,0:T(8,128)(2,1)}, bf16[3,1024,512]{2,1,0:T(8,128)(2,1)}, u32[]{:S(2)}, u32[]{:S(2)}) collective-permute-start(bf16[3,1024,512]{2,1,0:T(8,128)(2,1)} %bitcast.57), channel_id=1, source_target_pairs={{0,64},{64,0},{1,65},{65,1},{2,66},{66,2},{3,67},{67,3},{4,68},{68... | collective-permute-start | bytes 9437192 | tf_op jit(solution)/shard_map/ppermute | solution.py:399
  0.7 24.8 %collective-permute-start.8 = (bf16[1024,1024]{1,0:T(8,128)(2,1)}, bf16[1024,1024]{1,0:T(8,128)(2,1)}, u32[]{:S(2)}, u32[]{:S(2)}) collective-permute-start(bf16[1024,1024]{1,0:T(8,128)(2,1)} %bitcast.58), channel_id=1, source_target_pairs={{0,64},{64,0},{1,65},{65,1},{2,66},{66,2},{3,67},{67,3},{4,68},{68... | collective-permute-start | bytes 6291464 | tf_op jit(solution)/shard_map/ppermute | solution.py:399
  1.2 9.0 %collective-permute-start = (bf16[128,1024]{1,0:T(8,128)(2,1)}, bf16[128,1024]{1,0:T(8,128)(2,1)S(1)}, u32[]{:S(2)}, u32[]{:S(2)}) collective-permute-start(bf16[128,1024]{1,0:T(8,128)(2,1)} %bitcast.63), channel_id=1, source_target_pairs={{64,32},{65,33},{66,34},{67,35},{68,36},{69,37},{70,38},{71,39},{7... | collective-permute-start | bytes 786440 | tf_op jit(solution)/shard_map/ppermute | solution.py:405
  1.9 9.0 %collective-permute-start.1 = (bf16[128,1024]{1,0:T(8,128)(2,1)}, bf16[128,1024]{1,0:T(8,128)(2,1)S(1)}, u32[]{:S(2)}, u32[]{:S(2)}) collective-permute-start(bf16[128,1024]{1,0:T(8,128)(2,1)} %bitcast.64), channel_id=1, source_target_pairs={{64,0},{96,64},{65,1},{97,65},{66,2},{98,66},{67,3},{99,67},{68,4}... | collective-permute-start | bytes 786440 | tf_op jit(solution)/shard_map/ppermute | solution.py:404
  9.8 14.1 %collective-permute-start.6 = (bf16[512,1024]{1,0:T(8,128)(2,1)}, bf16[512,1024]{1,0:T(8,128)(2,1)}, u32[]{:S(2)}, u32[]{:S(2)}) collective-permute-start(bf16[512,1024]{1,0:T(8,128)(2,1)} %bitcast.62), channel_id=1, source_target_pairs={{0,64},{64,0},{1,65},{65,1},{2,66},{66,2},{3,67},{67,3},{4,68},{68... | collective-permute-start | bytes 3145736 | tf_op jit(solution)/shard_map/ppermute | solution.py:399
  10.9 30.9 %collective-permute-start.9 = (bf16[1024,1024]{1,0:T(8,128)(2,1)}, bf16[1024,1024]{1,0:T(8,128)(2,1)}, u32[]{:S(2)}, u32[]{:S(2)}) collective-permute-start(bf16[1024,1024]{1,0:T(8,128)(2,1)} %bitcast.59), channel_id=1, source_target_pairs={{0,64},{64,0},{1,65},{65,1},{2,66},{66,2},{3,67},{67,3},{4,68},{68... | collective-permute-start | bytes 6291464 | tf_op jit(solution)/shard_map/ppermute | solution.py:399
  14.8 8.1 %collective-permute-start.3 = (bf16[128,1024]{1,0:T(8,128)(2,1)}, bf16[128,1024]{1,0:T(8,128)(2,1)S(1)}, u32[]{:S(2)}, u32[]{:S(2)}) collective-permute-start(bf16[128,1024]{1,0:T(8,128)(2,1)} %bitcast.66), channel_id=1, source_target_pairs={{0,32},{32,64},{1,33},{33,65},{2,34},{34,66},{3,35},{35,67},{4,36}... | collective-permute-start | bytes 786440 | tf_op jit(solution)/shard_map/ppermute | solution.py:386
  39.3 8.5 %collective-permute-start.7 = (bf16[128,1024]{1,0:T(8,128)(2,1)S(1)}, bf16[128,1024]{1,0:T(8,128)(2,1)S(1)}, u32[]{:S(2)}, u32[]{:S(2)}) collective-permute-start(bf16[128,1024]{1,0:T(8,128)(2,1)S(1)} %get-tuple-element.63), channel_id=1, source_target_pairs={{0,32},{32,0},{1,33},{33,1},{2,34},{34,2},{3,35},{35,3},{4,36},{36... | collective-permute-start | bytes 786440 | tf_op jit(solution)/shard_map/ppermute | solution.py:414
  51.2 7.2 %collective-permute-start.10 = (bf16[128,1024]{1,0:T(8,128)(2,1)S(1)}, bf16[128,1024]{1,0:T(8,128)(2,1)S(1)}, u32[]{:S(2)}, u32[]{:S(2)}) collective-permute-start(bf16[128,1024]{1,0:T(8,128)(2,1)S(1)} %get-tuple-element.66), channel_id=1, source_target_pairs={{0,32},{32,0},{1,33},{33,1},{2,34},{34,2},{3,35},{35,3},{4,36},{36... | collective-permute-start | bytes 786440 | tf_op jit(solution)/shard_map/ppermute | solution.py:414
  65.1 6.4 %collective-permute-start.11 = (bf16[128,1024]{1,0:T(8,128)(2,1)S(1)}, bf16[128,1024]{1,0:T(8,128)(2,1)S(1)}, u32[]{:S(2)}, u32[]{:S(2)}) collective-permute-start(bf16[128,1024]{1,0:T(8,128)(2,1)S(1)} %get-tuple-element.69), channel_id=1, source_target_pairs={{0,32},{32,0},{1,33},{33,1},{2,34},{34,2},{3,35},{35,3},{4,36},{36... | collective-permute-start | bytes 786440 | tf_op jit(solution)/shard_map/ppermute | solution.py:414
  84.7 54.0 %all-to-all-start.6 = ((bf16[32,32,1024]{2,1,0:T(8,128)(2,1)}), bf16[32,32,1024]{2,1,0:T(8,128)(2,1)}, u32[]{:S(2)}, u32[]{:S(2)}) async-start(bf16[32,32,1024]{2,1,0:T(8,128)(2,1)} %bitcast.25), calls=%async_computation.6 | async-start | bytes 4194304 | tf_op jit(solution)/shard_map/all_to_all | solution.py:362
  95.5 28.3 %collective-permute-start.12 = (bf16[128,1024]{1,0:T(8,128)(2,1)S(1)}, bf16[128,1024]{1,0:T(8,128)(2,1)S(1)}, u32[]{:S(2)}, u32[]{:S(2)}) collective-permute-start(bf16[128,1024]{1,0:T(8,128)(2,1)S(1)} %get-tuple-element.74), channel_id=1, source_target_pairs={{0,32},{32,0},{1,33},{33,1},{2,34},{34,2},{3,35},{35,3},{4,36},{36... | collective-permute-start | bytes 786440 | tf_op jit(solution)/shard_map/ppermute | solution.py:414
  138.6 54.9 %all-to-all-start.2 = ((bf16[32,64,512]{2,1,0:T(8,128)(2,1)}), bf16[32,64,512]{2,1,0:T(8,128)(2,1)}, u32[]{:S(2)}, u32[]{:S(2)}) async-start(bf16[32,64,512]{2,1,0:T(8,128)(2,1)} %bitcast.16), calls=%async_computation.2 | async-start | bytes 4194304 | tf_op jit(solution)/shard_map/all_to_all | solution.py:362
  153.2 28.3 %collective-permute-start.13 = (bf16[128,1024]{1,0:T(8,128)(2,1)S(1)}, bf16[128,1024]{1,0:T(8,128)(2,1)S(1)}, u32[]{:S(2)}, u32[]{:S(2)}) collective-permute-start(bf16[128,1024]{1,0:T(8,128)(2,1)S(1)} %get-tuple-element.82), channel_id=1, source_target_pairs={{0,32},{32,0},{1,33},{33,1},{2,34},{34,2},{3,35},{35,3},{4,36},{36... | collective-permute-start | bytes 786440 | tf_op jit(solution)/shard_map/ppermute | solution.py:414
  193.6 56.7 %all-to-all-start.4 = ((bf16[32,32,1024]{2,1,0:T(8,128)(2,1)}), bf16[32,32,1024]{2,1,0:T(8,128)(2,1)}, u32[]{:S(2)}, u32[]{:S(2)}) async-start(bf16[32,32,1024]{2,1,0:T(8,128)(2,1)} %bitcast.22), calls=%async_computation.4 | async-start | bytes 4194304 | tf_op jit(solution)/shard_map/all_to_all | solution.py:362
  207.5 28.3 %collective-permute-start.14 = (bf16[128,1024]{1,0:T(8,128)(2,1)S(1)}, bf16[128,1024]{1,0:T(8,128)(2,1)S(1)}, u32[]{:S(2)}, u32[]{:S(2)}) collective-permute-start(bf16[128,1024]{1,0:T(8,128)(2,1)S(1)} %get-tuple-element.88), channel_id=1, source_target_pairs={{0,32},{32,0},{1,33},{33,1},{2,34},{34,2},{3,35},{35,3},{4,36},{36... | collective-permute-start | bytes 786440 | tf_op jit(solution)/shard_map/ppermute | solution.py:414
  250.3 45.9 %all-to-all-start = ((bf16[32,64,512]{2,1,0:T(8,128)(2,1)}), bf16[32,64,512]{2,1,0:T(8,128)(2,1)}, u32[]{:S(2)}, u32[]{:S(2)}) async-start(bf16[32,64,512]{2,1,0:T(8,128)(2,1)} %bitcast.12), calls=%async_computation | async-start | bytes 4194304 | tf_op jit(solution)/shard_map/all_to_all | solution.py:362
  297.8 33.9 %all-to-all-start.7 = ((bf16[32,32,1024]{2,1,0:T(8,128)(2,1)}), bf16[32,32,1024]{2,1,0:T(8,128)(2,1)S(1)}, u32[]{:S(2)}, u32[]{:S(2)}) async-start(bf16[32,32,1024]{2,1,0:T(8,128)(2,1)} %broadcast_in_dim.18), calls=%async_computation.7 | async-start | bytes 4194304 | tf_op jit(solution)/shard_map/all_to_all | solution.py:365
  333.4 33.5 %all-to-all-start.3 = ((bf16[32,64,512]{2,1,0:T(8,128)(2,1)}), bf16[32,64,512]{2,1,0:T(8,128)(2,1)}, u32[]{:S(2)}, u32[]{:S(2)}) async-start(bf16[32,64,512]{2,1,0:T(8,128)(2,1)} %broadcast_in_dim.16), calls=%async_computation.3 | async-start | bytes 4194304 | tf_op jit(solution)/shard_map/all_to_all | solution.py:365
  368.6 35.4 %all-to-all-start.5 = ((bf16[32,32,1024]{2,1,0:T(8,128)(2,1)}), bf16[32,32,1024]{2,1,0:T(8,128)(2,1)}, u32[]{:S(2)}, u32[]{:S(2)}) async-start(bf16[32,32,1024]{2,1,0:T(8,128)(2,1)} %broadcast_in_dim.17), calls=%async_computation.5 | async-start | bytes 4194304 | tf_op jit(solution)/shard_map/all_to_all | solution.py:365
  373.3 37.2 %collective-permute-start.15 = (bf16[128,1024]{1,0:T(8,128)(2,1)}, bf16[128,1024]{1,0:T(8,128)(2,1)S(1)}, u32[]{:S(2)}, u32[]{:S(2)}) collective-permute-start(bf16[128,1024]{1,0:T(8,128)(2,1)} %get-tuple-element.95), channel_id=1, source_target_pairs={{0,32},{32,0},{1,33},{33,1},{2,34},{34,2},{3,35},{35,3},{4,36},{36... | collective-permute-start | bytes 786440 | tf_op jit(solution)/shard_map/ppermute | solution.py:414
  405.6 55.4 %all-to-all-start.1 = ((bf16[32,64,512]{2,1,0:T(8,128)(2,1)}), bf16[32,64,512]{2,1,0:T(8,128)(2,1)}, u32[]{:S(2)}, u32[]{:S(2)}) async-start(bf16[32,64,512]{2,1,0:T(8,128)(2,1)} %broadcast_in_dim.15), calls=%async_computation.1 | async-start | bytes 4194304 | tf_op jit(solution)/shard_map/all_to_all | solution.py:365
  411.1 5.2 %collective-permute-start.22 = (f32[8,1024]{1,0:T(8,128)S(1)}, f32[8,1024]{1,0:T(8,128)S(1)}, u32[]{:S(2)}, u32[]{:S(2)}) collective-permute-start(f32[8,1024]{1,0:T(8,128)S(1)} %broadcast_select_fusion.10), channel_id=1, source_target_pairs={{0,64},{64,0},{1,65},{65,1},{2,66},{66,2},{3,67},{67,3},{4,68},{68... | collective-permute-start | bytes 98312 | tf_op jit(solution)/shard_map/ppermute | solution.py:417
  411.2 31.5 %collective-permute-start.16 = (bf16[128,1024]{1,0:T(8,128)(2,1)}, bf16[128,1024]{1,0:T(8,128)(2,1)S(1)}, u32[]{:S(2)}, u32[]{:S(2)}) collective-permute-start(bf16[128,1024]{1,0:T(8,128)(2,1)} %copy-done.41), channel_id=1, source_target_pairs={{0,32},{32,0},{1,33},{33,1},{2,34},{34,2},{3,35},{35,3},{4,36},{36... | collective-permute-start | bytes 786440 | tf_op jit(solution)/shard_map/ppermute | solution.py:414
  416.3 14.6 %collective-permute-start.23 = (f32[8,1024]{1,0:T(8,128)S(1)}, f32[8,1024]{1,0:T(8,128)S(1)}, u32[]{:S(2)}, u32[]{:S(2)}) collective-permute-start(f32[8,1024]{1,0:T(8,128)S(1)} %select_add_fusion), channel_id=1, source_target_pairs={{0,8},{8,0},{16,24},{24,16},{1,9},{9,1},{17,25},{25,17},{2,10},{10... | collective-permute-start | bytes 98312 | tf_op jit(solution)/shard_map/ppermute | solution.py:490
  436.0 35.9 %collective-permute-start.31 = (bf16[2,512,1024]{2,1,0:T(8,128)(2,1)}, bf16[2,512,1024]{2,1,0:T(8,128)(2,1)}, u32[]{:S(2)}, u32[]{:S(2)}) collective-permute-start(bf16[2,512,1024]{2,1,0:T(8,128)(2,1)} %bitcast.50), channel_id=1, source_target_pairs={{0,64},{1,65},{2,66},{3,67},{4,68},{5,69},{6,70},{7,71},{8,72},{9,... | collective-permute-start | bytes 6291464 | tf_op jit(solution)/shard_map/ppermute | solution.py:468
  445.0 7.3 %collective-permute-start.27 = (f32[8,1024]{1,0:T(8,128)S(1)}, f32[8,1024]{1,0:T(8,128)S(1)}, u32[]{:S(2)}, u32[]{:S(2)}) collective-permute-start(f32[8,1024]{1,0:T(8,128)S(1)} %add.57), channel_id=1, source_target_pairs={{0,1},{1,0},{2,3},{3,2},{4,5},{5,4},{6,7},{7,6},{8,9},{9,8},{10,11... | collective-permute-start | bytes 98312 | tf_op jit(solution)/shard_map/ppermute | solution.py:490
  448.3 25.4 %collective-permute-start.21 = (bf16[4,512,512]{2,1,0:T(8,128)(2,1)}, bf16[4,512,512]{2,1,0:T(8,128)(2,1)}, u32[]{:S(2)}, u32[]{:S(2)}) collective-permute-start(bf16[4,512,512]{2,1,0:T(8,128)(2,1)} %bitcast.17), channel_id=1, source_target_pairs={{0,64},{1,65},{2,66},{3,67},{4,68},{5,69},{6,70},{7,71},{8,72},{9,... | collective-permute-start | bytes 6291464 | tf_op jit(solution)/shard_map/ppermute | solution.py:468
  451.0 11.3 %collective-permute-start.17 = (f32[128,1024]{1,0:T(8,128)S(1)}, f32[128,1024]{1,0:T(8,128)S(1)}, u32[]{:S(2)}, u32[]{:S(2)}) collective-permute-start(f32[128,1024]{1,0:T(8,128)S(1)} %broadcast_select_fusion.8), channel_id=1, source_target_pairs={{0,64},{96,32},{1,65},{97,33},{2,66},{98,34},{3,67},{99,35},{4,68}... | collective-permute-start | bytes 1572872 | tf_op jit(solution)/shard_map/ppermute | solution.py:494
  452.3 7.4 %collective-permute-start.32 = (f32[6,1024]{1,0:T(8,128)S(1)}, f32[6,1024]{1,0:T(8,128)S(1)}, u32[]{:S(2)}, u32[]{:S(2)}) collective-permute-start(f32[6,1024]{1,0:T(8,128)S(1)} %slice.118), channel_id=1, source_target_pairs={{0,32},{32,0},{1,33},{33,1},{2,34},{34,2},{3,35},{35,3},{4,36},{36... | collective-permute-start | bytes 73736 | tf_op jit(solution)/shard_map/ppermute | solution.py:414
  458.5 17.8 %collective-permute-start.29 = (bf16[2,512,1024]{2,1,0:T(8,128)(2,1)}, bf16[2,512,1024]{2,1,0:T(8,128)(2,1)}, u32[]{:S(2)}, u32[]{:S(2)}) collective-permute-start(bf16[2,512,1024]{2,1,0:T(8,128)(2,1)} %bitcast.24), channel_id=1, source_target_pairs={{64,0},{65,1},{66,2},{67,3},{68,4},{69,5},{70,6},{71,7},{72,8},{73... | collective-permute-start | bytes 6291464 | tf_op jit(solution)/shard_map/ppermute | solution.py:468
  461.0 21.4 %collective-permute-start.19 = (bf16[4,512,512]{2,1,0:T(8,128)(2,1)}, bf16[4,512,512]{2,1,0:T(8,128)(2,1)S(1)}, u32[]{:S(2)}, u32[]{:S(2)}) collective-permute-start(bf16[4,512,512]{2,1,0:T(8,128)(2,1)} %bitcast.14), channel_id=1, source_target_pairs={{64,0},{65,1},{66,2},{67,3},{68,4},{69,5},{70,6},{71,7},{72,8},{73... | collective-permute-start | bytes 6291464 | tf_op jit(solution)/shard_map/ppermute | solution.py:468
  (56 other events, 606.4 us)
where the time goes:
time: 493 us; the launch traced here: 487 us
  waiting for transfers between devices  242 us (49%)
  starting transfers between devices  120 us (24%)
  Pallas kernels  47.9 us (10%)
  local copies, waits for them, and re-layouts  39.8 us (8%)
  other arithmetic  34.6 us (7%)
    ppermute x9, waiting for transfers between devices, swapped(): return lax.ppermute(sent, 'tensor', SWAP)  99.6 us
    all_to_all x4, waiting for transfers between devices, reduced(): return lax.all_to_all(spread, DP, split_axis=0, concat_axis=0, tiled=True)  79.2 us
    all_to_all x4, starting transfers between devices, reduced(): pieces = lax.all_to_all(pieces, DP, split_axis=0, concat_axis=0, tiled=True)  53.2 us
    pallas_call x14, Pallas kernels, call(): pl.pallas_call(body, name=name, in_specs=[smem] * scalars + [vmem] * (len...  47.9 us
    all_to_all x4, waiting for transfers between devices, reduced(): pieces = lax.all_to_all(pieces, DP, split_axis=0, concat_axis=0, tiled=True)  29.9 us
    ppermute x5, waiting for transfers between devices, local(): vectors = vectors + lax.ppermute(vectors, axis, pairs)  20.2 us
    all_to_all x4, starting transfers between devices, reduced(): return lax.all_to_all(spread, DP, split_axis=0, concat_axis=0, tiled=True)  18.5 us
    ppermute x9, starting transfers between devices, swapped(): return lax.ppermute(sent, 'tensor', SWAP)  17.8 us
  transfers between devices with their start and end apart: 41, of which 20 were waited for; matrix products, arithmetic and copies ran while one was open for 10% of the time, Pallas kernels for 6%

commit v1 on v0

--- a/solution.py
+++ b/solution.py
@@ -15,10 +15,7 @@
 bf16 = jnp.bfloat16
 
 SWAP = ((0, 1), (1, 0))
-PAIR_E = ((0, 1), (1, 0), (2, 3), (3, 2))
-PAIR_F = ((0, 3), (3, 0), (1, 2), (2, 1))
 DP = ("y", "z", "xh")
-ROUNDS = (("y", PAIR_E), ("y", PAIR_F), ("z", PAIR_E), ("z", PAIR_F), ("xh", SWAP))
 
 
 GELU_A = 0.7978845608028654
@@ -281,14 +278,123 @@
     out_ref[512:, :] = matmul_tn(left, right).astype(bf16)
 
 
-def attention_weight_grads(core, context, resid_half, attn_rows, proj_grad, crossed, out_ref):
+def attention_weight_grads(core, context, resid_half, attn_rows, proj_grad, crossed, _, out_ref):
     left = stacked(halves(core, attn_rows[...])[0], crossed[:, 1024:1536])
     for c in range(3):
         far = crossed[:, 1536 + c * LOCAL : 1536 + (c + 1) * LOCAL]
-        out_ref[c * 512 : (c + 1) * 512, :] = matmul_tn(left, stacked(proj_grad[c], far)).astype(bf16)
+        spot = (slice(512 * (c // 2), 512 * (c // 2 + 1)), slice(512 * (c % 2), 512 * (c % 2 + 1)))
+        out_ref[spot] = matmul_tn(left, stacked(proj_grad[c], far)).astype(bf16)
     left = stacked(context[...], crossed[:, :512])
     right = stacked(halves(core, resid_half[...])[0], crossed[:, 512:1024])
-    out_ref[1536:, :] = matmul_tn(left, right).astype(bf16)
+    out_ref[512:, 512:] = matmul_tn(left, right).astype(bf16)
+
+
+def pack_kernel(body, name, place):
+    def whole(operand):
+        zeros = (0,) * operand.ndim
+        return pl.BlockSpec(operand.shape, lambda i: zeros)
+
+    def call(core_length, *operands):
+        specs = [whole(operand) for operand in operands]
+        if place:
+            specs[-1] = pl.BlockSpec(memory_space=pl.ANY)
+        return pl.pallas_call(
+            body,
+            name=name,
+            grid=(1,),
+            in_specs=[pl.BlockSpec(memory_space=pltpu.SMEM)] + specs,
+            out_specs=pl.BlockSpec((1024, WIDTH), lambda i: (place, 0)),
+            out_shape=jax.ShapeDtypeStruct((2048, WIDTH), bf16),
+            input_output_aliases={len(operands): 0} if place else {},
+            compiler_params=pltpu.CompilerParams(vmem_limit_bytes=48 * 1024 * 1024),
+        )(core_length, *operands)
+
+    return call
+
+
+RANKS = 32
+CHUNK = 2048 // RANKS
+
+
+def sum_spread(pieces, out_ref):
+    total = pieces[0].astype(f32)
+    for rank in range(1, RANKS):
+        total = total + pieces[rank].astype(f32)
+    out_ref[...] = jnp.broadcast_to(total.astype(bf16)[None], out_ref.shape)
+
+
+def sum_and_spread(pieces):
+    block = pl.BlockSpec((RANKS, 16, WIDTH), lambda i: (0, i, 0))
+    return pl.pallas_call(
+        sum_spread,
+        name="sum_and_spread",
+        grid=(CHUNK // 16,),
+        in_specs=[block],
+        out_specs=block,
+        out_shape=jax.ShapeDtypeStruct(pieces.shape, bf16),
+        compiler_params=pltpu.CompilerParams(vmem_limit_bytes=48 * 1024 * 1024),
+    )(pieces)
+
+
+def assemble_body(core, *refs):
+    packs = [refs[4 * i : 4 * i + 4] for i in range(4)]
+    qkv_ref, out_ref, up_ref, down_ref = refs[16:]
+    low_core = core[0] == 0
+    low_half = pl.program_id(0) == 0
+
+    def piece(segment):
+        mine_0, theirs_0, mine_1, theirs_1 = (pack[segment][...] for pack in packs)
+        at_0 = jnp.where(low_half, mine_0, theirs_0)
+        at_1 = jnp.where(low_half, theirs_1, mine_1)
+        return jnp.where(low_core, at_0, at_1).reshape(2 * CHUNK, WIDTH).astype(f32)
+
+    down_ref[...] = piece(0)
+    up_ref[...] = piece(1)
+    block = piece(2)
+    qkv_ref[0] = block[:, :512]
+    qkv_ref[1] = block[:, 512:]
+    block = piece(3)
+    qkv_ref[2] = block[:, :512]
+    out_ref[...] = block[:, 512:]
+
+
+def assemble(core_length, mine_0, theirs_0, mine_1, theirs_1):
+    def spec(segment, layer, half):
+        def index(h, q, core):
+            live = (core[0] == layer) & (h == half)
+            return (segment * 4 + jnp.where(live, q, 0), 0, 0)
+
+        return pl.BlockSpec((2, CHUNK, WIDTH), index)
+
+    operands = []
+    specs = []
+    for array, layer, half in ((mine_0, 0, 0), (theirs_0, 0, 1), (mine_1, 1, 1), (theirs_1, 1, 0)):
+        for segment in range(4):
+            operands.append(array)
+            specs.append(spec(segment, layer, half))
+    rows = pl.BlockSpec((2 * CHUNK, WIDTH), lambda h, q, core: (4 * h + q, 0))
+    return pl.pallas_call(
+        assemble_body,
+        name="assemble",
+        grid_spec=pltpu.PrefetchScalarGridSpec(
+            num_scalar_prefetch=1,
+            grid=(2, 4),
+            in_specs=specs,
+            out_specs=[
+                pl.BlockSpec((3, 2 * CHUNK, 512), lambda h, q, core: (0, 4 * h + q, 0)),
+                pl.BlockSpec((2 * CHUNK, 512), lambda h, q, core: (q, h)),
+                rows,
+                rows,
+            ],
+        ),
+        out_shape=[
+            jax.ShapeDtypeStruct((3, 1024, 512), f32),
+            jax.ShapeDtypeStruct((512, 1024), f32),
+            jax.ShapeDtypeStruct((1024, 1024), f32),
+            jax.ShapeDtypeStruct((1024, 1024), f32),
+        ],
+        compiler_params=pltpu.CompilerParams(vmem_limit_bytes=48 * 1024 * 1024),
+    )(core_length, *operands)
 
 
 def device_kernel(body, name, scalars, shapes):
@@ -349,20 +455,12 @@
     ),
 )
 LAST_INPUT_GRAD = device_kernel(last_input_grad, "last_input_grad", 0, ((ROWS, f32), TABLE))
-MLP_WEIGHT_GRADS = device_kernel(mlp_weight_grads, "mlp_weight_grads", 1, (((1024, 1024), bf16),))
-ATTENTION_WEIGHT_GRADS = device_kernel(
-    attention_weight_grads, "attention_weight_grads", 1, (((2048, 512), bf16),)
-)
-
-
-def reduced(packed):
-    ranks = lax.axis_size(DP)
-    rows, columns = packed.shape
-    pieces = packed.reshape(ranks, rows // ranks, columns)
-    pieces = lax.all_to_all(pieces, DP, split_axis=0, concat_axis=0, tiled=True)
-    total = jnp.sum(pieces.astype(f32), axis=0).astype(bf16)
-    spread = jnp.broadcast_to(total[None], (ranks,) + total.shape)
-    return lax.all_to_all(spread, DP, split_axis=0, concat_axis=0, tiled=True)
+MLP_WEIGHT_GRADS = pack_kernel(mlp_weight_grads, "mlp_weight_grads", 0)
+ATTENTION_WEIGHT_GRADS = pack_kernel(attention_weight_grads, "attention_weight_grads", 1)
+
+
+def exchange(pieces):
+    return lax.all_to_all(pieces, DP, split_axis=0, concat_axis=0, tiled=True)
 
 
 def local(
@@ -385,7 +483,6 @@
     own_rows = section_in[0, 0, 0]
     near = lax.ppermute(own_rows, both, ((0, 1), (1, 2)))
     far = lax.ppermute(own_rows, both, ((1, 3),))
-    layer_in = jnp.where(place == 0, own_rows, jnp.where(place == 3, far, near))
 
     table = jnp.concatenate(
         [
@@ -396,15 +493,17 @@
         ]
     )
     owned = (qkv_weight[0], out_weight[0], up_weight[0], down_weight[0], table)
-    other = tuple(lax.ppermute(array, "pipe", SWAP) for array in owned)
+    first_far = [lax.ppermute(array, "pipe", SWAP) for array in (qkv_weight[0], out_weight[0], table)]
+    up_own, down_own, near, far, *first_far = lax.optimization_barrier(
+        (up_weight[0], down_weight[0], near, far, *first_far)
+    )
+    layer_in = jnp.where(place == 0, own_rows, jnp.where(place == 3, far, near))
+    second_far = [lax.ppermute(array, "pipe", SWAP) for array in (up_own, down_own)]
+    other = (first_far[0], first_far[1], second_far[0], second_far[1], first_far[2])
     layers = tuple(
         tuple(jnp.where(core == layer, mine, theirs) for mine, theirs in zip(owned, other))
         for layer in range(2)
     )
-    cot_near = lax.ppermute(own_rows, both, ((2, 0), (3, 2)))
-    cot_far = lax.ppermute(own_rows, both, ((2, 1),))
-    cotangent = jnp.where(place == 3, own_rows, jnp.where(place == 1, cot_far, cot_near))
-
     seq_length = jnp.where(core == 0, lengths[0, 0], lengths[0, 1])
     core_length = jnp.stack([core, seq_length]).astype(jnp.int32)
     head_ids = tensor_index * HEADS_DEV + jnp.arange(HEADS_DEV) + 1
@@ -423,8 +522,12 @@
     attn_0, proj_0, prob_0, context_0, part, sent = FIRST_ATTENTION(
         core_length, slopes, rows_0, table_0, qkv_0, out_0
     )
+    received, cot_own = lax.optimization_barrier((swapped(sent), own_rows))
+    cot_near = lax.ppermute(cot_own, both, ((2, 0), (3, 2)))
+    cot_far = lax.ppermute(cot_own, both, ((2, 1),))
+    cotangent = jnp.where(place == 3, own_rows, jnp.where(place == 1, cot_far, cot_near))
     resid_0, mlp_0, pre_0, act_0, part, sent = MLP_FORWARD(
-        rows_0, part, swapped(sent), table_0, up_0, down_0
+        rows_0, part, received, table_0, up_0, down_0
     )
     _, rows_1, attn_1, proj_1, prob_1, context_1, part, sent = NEXT_ATTENTION(
         core_length, slopes, resid_0, part, swapped(sent), table_0, table_1, qkv_1, out_1
@@ -437,66 +540,61 @@
     pre_half_1, part, sent, cross_mlp, sums_mlp_1 = MLP_BACKWARD(
         core_length, cotangent, pre_1, act_1, mlp_1, up_1, down_1
     )
-    (early_1,) = MLP_WEIGHT_GRADS(
+    pack_1 = MLP_WEIGHT_GRADS(
         core_length, act_1, cotangent, mlp_1, pre_half_1, crossed(cross_mlp)
     )
+    received, pack_1, out_one = lax.optimization_barrier((swapped(sent), pack_1, out_one))
     grad_1, resid_half_1, proj_grad_1, part, sent, cross_attn, sums_attn_1 = ATTENTION_BACKWARD(
-        core_length, cotangent, part, swapped(sent), resid_1, table_1, out_1, qkv_1,
+        core_length, cotangent, part, received, resid_1, table_1, out_1, qkv_1,
         proj_1, prob_1, context_1, attn_1,
     )
-    (late_1,) = ATTENTION_WEIGHT_GRADS(
-        core_length, context_1, resid_half_1, attn_1, proj_grad_1, crossed(cross_attn)
-    )
+    pack_1 = ATTENTION_WEIGHT_GRADS(
+        core_length, context_1, resid_half_1, attn_1, proj_grad_1, crossed(cross_attn), pack_1
+    )
+    received, pack_1 = lax.optimization_barrier((swapped(sent), pack_1))
     grad_half, sums_in_1, pre_half_0, part, sent, cross_mlp, sums_mlp_0 = MLP_BACKWARD_BELOW(
-        core_length, grad_1, part, swapped(sent), rows_1, table_1,
+        core_length, grad_1, part, received, rows_1, table_1,
         pre_0, act_0, mlp_0, up_0, down_0,
     )
-    (early_0,) = MLP_WEIGHT_GRADS(
+    pack_0 = MLP_WEIGHT_GRADS(
         core_length, act_0, grad_half, mlp_0, pre_half_0, crossed(cross_mlp)
     )
+    received, pack_0 = lax.optimization_barrier((swapped(sent), pack_0))
     grad_0, resid_half_0, proj_grad_0, part, sent, cross_attn, sums_attn_0 = ATTENTION_BACKWARD(
-        core_length, grad_half, part, swapped(sent), resid_0, table_0, out_0, qkv_0,
+        core_length, grad_half, part, received, resid_0, table_0, out_0, qkv_0,
         proj_0, prob_0, context_0, attn_0,
     )
-    (late_0,) = ATTENTION_WEIGHT_GRADS(
-        core_length, context_0, resid_half_0, attn_0, proj_grad_0, crossed(cross_attn)
-    )
-    grad_zero, sums_in_0 = LAST_INPUT_GRAD(grad_0, part, swapped(sent), rows_0, table_0)
-
-    def weights_of(layer, early, late):
-        def both_halves(mine):
-            theirs = lax.ppermute(mine, "pipe", ((1 - layer, layer),))
-            return (mine, theirs) if layer == 0 else (theirs, mine)
-
-        early = both_halves(reduced(early).reshape(2, 512, 1024))
-        late = both_halves(reduced(late).reshape(4, 512, 512))
-        return (
-            jnp.concatenate([half[:3] for half in late], axis=1),
-            jnp.concatenate([half[3] for half in late], axis=1),
-            jnp.concatenate([half[1] for half in early], axis=0),
-            jnp.concatenate([half[0] for half in early], axis=0),
-        )
-
-    weights_one = weights_of(1, early_1, late_1)
-    weights_zero = weights_of(0, early_0, late_0)
+    pack_0 = ATTENTION_WEIGHT_GRADS(
+        core_length, context_0, resid_half_0, attn_0, proj_grad_0, crossed(cross_attn), pack_0
+    )
+    received = swapped(sent)
+    received, pack_1, pack_0 = lax.optimization_barrier((received, pack_1, pack_0))
+    grad_zero, sums_in_0 = LAST_INPUT_GRAD(grad_0, part, received, rows_0, table_0)
+
     vectors_one = sums_in_1 + sums_mlp_1 + sums_attn_1
     vectors_zero = sums_in_0 + sums_mlp_0 + sums_attn_0
-
     first = core == 0
     vectors = jnp.where(first, vectors_zero, vectors_one) + crossed(
         jnp.where(first, vectors_one, vectors_zero)
     )
-    for axis, pairs in ROUNDS:
-        vectors = vectors + lax.ppermute(vectors, axis, pairs)
-    shared = vectors[2:]
+    shared = vectors[GAIN_A:]
     shared = 0.5 * (shared + swapped(shared))
-
+    vectors = jnp.concatenate([vectors[:GAIN_A], shared])
+
+    pieces_1 = exchange(pack_1.reshape(RANKS, CHUNK, WIDTH))
+    pieces_0 = exchange(pack_0.reshape(RANKS, CHUNK, WIDTH))
     crossing = lax.ppermute(jnp.where(first, out_one, grad_zero), both, ((0, 2), (3, 1)))
+    total_1 = jnp.sum(pieces_1.astype(f32), axis=0).astype(bf16)
+    total_1, crossing = lax.optimization_barrier((total_1, crossing))
+    mine_1 = lax.all_gather(jnp.concatenate([total_1, vectors.astype(bf16)]), DP, axis=0)
+    mine_0 = exchange(sum_and_spread(pieces_0))
+    theirs_1 = lax.ppermute(mine_1, "pipe", ((0, 1),))
+    theirs_0 = lax.ppermute(mine_0, "pipe", ((1, 0),))
+    qkv_g, out_g, up_g, down_g = assemble(core_length, mine_0, theirs_0, mine_1, theirs_1)
+    vectors = jnp.sum(mine_1[:, CHUNK:].astype(f32), axis=0)
+
     kept_rows = jnp.where(first, grad_zero, out_one)
     section_out = jnp.where(core == tensor_index, kept_rows, crossing)
-    qkv_g, out_g, up_g, down_g = (
-        jnp.where(first, zero, one).astype(f32) for zero, one in zip(weights_zero, weights_one)
-    )
     return (
         section_out[None, None, None],
         qkv_g[None],
@@ -505,8 +603,8 @@
         up_g[None],
         vectors[1][None],
         down_g[None],
-        shared[:2][None],
-        shared[2:][None],
+        vectors[2:4][None],
+        vectors[4:][None],
     )
 
 

time: 493 us -> 412 us (0.84)
  the two profiles are of different devices: /device:TPU:0 before, /device:TPU:67 now
where the time goes in v1:
time: 412 us; the launch traced here: 411 us
  waiting for transfers between devices  179 us (43%)
  blocking collectives  60.2 us (15%)
  Pallas kernels  59 us (14%)
  starting transfers between devices  51.5 us (12%)
  other arithmetic  24.9 us (6%)
  local copies, waits for them, and re-layouts  20.4 us (5%)
  between operations  16 us (4%)
    all_gather x1, waiting for transfers between devices, local(): lax.all_gather(jnp.concatenate([total_1, vectors.astype(bf16)]), DP, axis=0)  84.5 us
    ppermute x9, waiting for transfers between devices, swapped(): return lax.ppermute(sent, 'tensor', SWAP)  75.7 us
    all_to_all x1, blocking collectives, exchange(): return lax.all_to_all(pieces, DP, split_axis=0, concat_axis=0, tiled=True)  60.2 us
    pallas_call x10, Pallas kernels, call(): pl.pallas_call(body, name=name, in_specs=[smem] * scalars + [vmem] * (len...  37.6 us
    unnamed x99, local copies, waits for them, and re-layouts  16.7 us
    all_to_all x2, starting transfers between devices, exchange(): return lax.all_to_all(pieces, DP, split_axis=0, concat_axis=0, tiled=True)  16.6 us
    select_n x5, other arithmetic, local(): jnp.where(core == layer, mine, theirs)  14.5 us
    pallas_call x1, Pallas kernels, assemble(): pl.pallas_call(assemble_body, name='assemble', grid_spec=pltpu.PrefetchSc...  12.8 us
  transfers between devices with their start and end apart: 29, of which 17 were waited for; matrix products, arithmetic and copies ran while one was open for 6% of the time, Pallas kernels for 5%

profile of v1, /device:TPU:67, one launch (start us, length us, event | category | flops | bytes accessed | tf_op | source)
XLA Modules:
  0.0 411.0 jit_solution(18072798432738529196)
XLA Ops:
  24.2 5.8 %broadcast_select_fusion = (bf16[3,1024,512]{2,1,0:T(8,128)(2,1)}, bf16[3,1024,512]{2,1,0:T(8,128)(2,1)}) fusion(bf16[3,1024,512]{2,1,0:T(8,128)(2,1)} %collective-permute-done.2, pred[]{:T(512)S(6)} %eq.34, bf16[1,3,1024,512]{3,2,1,0:T(8,128)(2,1)S(1)} %copy-done.44, pred[]{:T(512)S(6)} %eq.13), kind=kLoop, calls=%fused_computation | loop fusion | flops 3145728 | bytes 12582914 | tf_op jit(solution)/shard_map/jit(_where)/select_n | solution.py:504
  29.9 5.4 %first_attention.1 = (bf16[128,1024]{1,0:T(8,128)(2,1)S(1)}, bf16[3,128,512]{2,1,0:T(8,128)(2,1)S(1)}, f32[8,128,128]{2,1,0:T(8,128)S(1)}, bf16[128,512]{1,0:T(8...) custom-call(s32[2]{0:T(128)S(1)} %pad_add_fusion.core, f32[8]{0:T(128)S(1)} %multiply_power_fusion.slopes, ...), custom_call_target="tpu_custom_call" | custom-call | tf_op jit(solution)/shard_map/first_attention/pallas_call | solution.py:405
  36.2 7.5 %collective-permute-done.5.received = bf16[128,1024]{1,0:T(8,128)(2,1)S(1)} collective-permute-done((bf16[128,1024]{1,0:T(8,128)(2,1)S(1)}, bf16[128,1024]{1,0:T(8,128)(2,1)S(1)}, u32[]{:S(2)}, u32[]{:S(2)}) %collective-permute-start.5) | collective-permute-done | bytes 262176 | tf_op jit(solution)/shard_map/ppermute | solution.py:513
  45.3 4.6 %broadcast_select_fusion.2 = (bf16[1024,1024]{1,0:T(8,128)(2,1)}, bf16[1024,1024]{1,0:T(8,128)(2,1)}) fusion(bf16[1024,1024]{1,0:T(8,128)(2,1)} %collective-permute-done.9, pred[]{:T(512)S(6)} %eq.34, bf16[1,1024,1024]{2,1,0:T(8,128)(2,1)S(1)} %copy-done.46, pred[]{:T(512)S(6)} %eq.13), kind=kLoop, calls=%fused_computation.2 | loop fusion | flops 2097152 | bytes 8388610 | tf_op jit(solution)/shard_map/jit(_where)/select_n | solution.py:504
  49.9 2.6 mlp_forward.2
  56.5 6.4 %collective-permute-start.7 = (bf16[128,1024]{1,0:T(8,128)(2,1)}, bf16[128,1024]{1,0:T(8,128)(2,1)}, u32[]{:S(2)}, u32[]{:S(2)}) collective-permute-start(bf16[128,1024]{1,0:T(8,128)(2,1)} %bitcast.4), channel_id=1, source_target_pairs={{64,0},{96,64},{65,1},{97,65},{66,2},{98,66},{67,3},{99,67},{68,4}... | collective-permute-start | bytes 786440 | tf_op jit(solution)/shard_map/ppermute | solution.py:526
  62.9 6.1 %next_attention.1 = (f32[128,1024]{1,0:T(8,128)}, bf16[128,1024]{1,0:T(8,128)(2,1)S(1)}, bf16[128,1024]{1,0:T(8,128)(2,1)S(1)}, bf16[3,128,512]{2,1,0:T(8,128)(2...) custom-call(s32[2]{0:T(128)S(1)} %pad_add_fusion.core, ...), custom_call_target="tpu_custom_call" | custom-call | tf_op jit(solution)/shard_map/next_attention/pallas_call | solution.py:405
  74.6 4.3 %collective-permute-done.11.received = bf16[128,1024]{1,0:T(8,128)(2,1)S(1)} collective-permute-done((bf16[128,1024]{1,0:T(8,128)(2,1)}, bf16[128,1024]{1,0:T(8,128)(2,1)S(1)}, u32[]{:S(2)}, u32[]{:S(2)}) %collective-permute-start.11) | collective-permute-done | bytes 262176 | tf_op jit(solution)/shard_map/ppermute | solution.py:513
  82.6 2.6 mlp_forward.3
  85.2 3.3 mlp_backward.1
  88.5 3.6 collective-permute-start.13
  93.6 6.4 %collective-permute-done.14.received = bf16[128,1024]{1,0:T(8,128)(2,1)S(1)} collective-permute-done((bf16[128,1024]{1,0:T(8,128)(2,1)S(1)}, bf16[128,1024]{1,0:T(8,128)(2,1)S(1)}, u32[]{:S(2)}, u32[]{:S(2)}) %collective-permute-start.14) | collective-permute-done | bytes 262176 | tf_op jit(solution)/shard_map/ppermute | solution.py:513
  101.4 4.2 %collective-permute-done.12.dc_received = bf16[128,1024]{1,0:T(8,128)(2,1)S(1)} collective-permute-done((bf16[128,1024]{1,0:T(8,128)(2,1)S(1)}, bf16[128,1024]{1,0:T(8,128)(2,1)S(1)}, u32[]{:S(2)}, u32[]{:S(2)}) %collective-permute-start.12) | collective-permute-done | bytes 262176 | tf_op jit(solution)/shard_map/ppermute | solution.py:513
  105.6 6.3 %attention_backward.2 = (f32[128,1024]{1,0:T(8,128)S(1)}, bf16[128,1024]{1,0:T(8,128)(2,1)S(1)}, bf16[3,128,512]{2,1,0:T(8,128)(2,1)S(1)}, f32[128,1024]{1,0:T(8...) custom-call(s32[2]{0:T(128)S(1)} %pad_add_fusion.core, ...), custom_call_target="tpu_custom_call" | custom-call | tf_op jit(solution)/shard_map/attention_backward/pallas_call | solution.py:405
  116.1 4.6 %collective-permute-done.15.da_received = bf16[128,1024]{1,0:T(8,128)(2,1)S(1)} collective-permute-done((bf16[128,1024]{1,0:T(8,128)(2,1)S(1)}, bf16[128,1024]{1,0:T(8,128)(2,1)S(1)}, u32[]{:S(2)}, u32[]{:S(2)}) %collective-permute-start.15) | collective-permute-done | bytes 262176 | tf_op jit(solution)/shard_map/ppermute | solution.py:513
  120.8 4.3 %mlp_backward_below.1 = (bf16[128,1024]{1,0:T(8,128)(2,1)S(1)}, f32[8,1024]{1,0:T(8,128)S(1)}, bf16[128,1024]{1,0:T(8,128)(2,1)S(1)}, f32[128,1024]{1,0:T(8,128)...) custom-call(s32[2]{0:T(128)S(1)} %pad_add_fusion.core, ...), custom_call_target="tpu_custom_call" | custom-call | tf_op jit(solution)/shard_map/mlp_backward_below/pallas_call | solution.py:405
  129.3 4.7 %collective-permute-done.17.dc_received = bf16[128,1024]{1,0:T(8,128)(2,1)S(1)} collective-permute-done((bf16[128,1024]{1,0:T(8,128)(2,1)S(1)}, bf16[128,1024]{1,0:T(8,128)(2,1)S(1)}, u32[]{:S(2)}, u32[]{:S(2)}) %collective-permute-start.17) | collective-permute-done | bytes 262176 | tf_op jit(solution)/shard_map/ppermute | solution.py:513
  134.0 6.3 %attention_backward.3 = (f32[128,1024]{1,0:T(8,128)S(1)}, bf16[128,1024]{1,0:T(8,128)(2,1)S(1)}, bf16[3,128,512]{2,1,0:T(8,128)(2,1)S(1)}, f32[128,1024]{1,0:T(8...) custom-call(s32[2]{0:T(128)S(1)} %pad_add_fusion.core, ...), custom_call_target="tpu_custom_call" | custom-call | tf_op jit(solution)/shard_map/attention_backward/pallas_call | solution.py:405
  145.2 2.0 copy-done.1
  147.3 2.7 collective-permute-done.19.received
  150.0 8.9 %all-to-all-start = ((bf16[32,64,1024]{2,1,0:T(8,128)(2,1)}), bf16[32,64,1024]{2,1,0:T(8,128)(2,1)}, u32[]{:S(2)}, u32[]{:S(2)}) async-start(bf16[32,64,1024]{2,1,0:T(8,128)(2,1)} %bitcast.37), calls=%async_computation | async-start | bytes 8388608 | tf_op jit(solution)/shard_map/all_to_all | solution.py:463
  159.6 3.3 collective-permute-start.21
  164.6 41.3 %collective-permute-done.24 = f32[6,1024]{1,0:T(8,128)S(1)} collective-permute-done((f32[6,1024]{1,0:T(8,128)S(1)}, f32[6,1024]{1,0:T(8,128)S(1)}, u32[]{:S(2)}, u32[]{:S(2)}) %collective-permute-start.24) | collective-permute-done | bytes 24608 | tf_op jit(solution)/shard_map/ppermute | solution.py:513
  205.9 10.1 %all-to-all-done = bf16[32,64,1024]{2,1,0:T(8,128)(2,1)} async-done(((bf16[32,64,1024]{2,1,0:T(8,128)(2,1)}), bf16[32,64,1024]{2,1,0:T(8,128)(2,1)}, u32[]{:S(2)}, u32[]{:S(2)}) %all-to-all-start) | async-done | bytes 4194336 | tf_op jit(solution)/shard_map/all_to_all | solution.py:463
  216.0 3.1 reduce_sum.21
  219.8 60.2 %all_to_all.15.pieces = bf16[32,64,1024]{2,1,0:T(8,128)(2,1)} all-to-all(bf16[32,64,1024]{2,1,0:T(8,128)(2,1)} %bitcast.38), channel_id=1, replica_groups=mesh['pipe'=2,'tensor'=2,'y'=4,'z'=4,'xh'=2] {'y','z','xh'}, dimensions={0} | all-to-all | bytes 8388608 | tf_op jit(solution)/shard_map/all_to_all | solution.py:463
  280.0 3.5 sum_and_spread.1
  283.5 2.0 copy-done.4
  285.5 7.7 %all-to-all-start.2 = ((bf16[32,64,1024]{2,1,0:T(8,128)(2,1)}), bf16[32,64,1024]{2,1,0:T(8,128)(2,1)}, u32[]{:S(2)}, u32[]{:S(2)}) async-start(bf16[32,64,1024]{2,1,0:T(8,128)(2,1)} %copy-done.4), calls=%async_computation.2 | async-start | bytes 8388608 | tf_op jit(solution)/shard_map/all_to_all | solution.py:463
  293.2 84.5 %all-gather.3.cloned.1.call-done = bf16[2304,1024]{1,0:T(8,128)(2,1)} async-done(((bf16[72,1024]{1,0:T(8,128)(2,1)}), bf16[2304,1024]{1,0:T(8,128)(2,1)}) %all-gather.3.cloned.1.call-update) | async-done | bytes 4718608 | tf_op jit(solution)/shard_map/all_gather | solution.py:589
  379.0 7.2 %collective-permute-start.22 = (bf16[32,64,1024]{2,1,0:T(8,128)(2,1)}, bf16[32,64,1024]{2,1,0:T(8,128)(2,1)}, u32[]{:S(2)}, u32[]{:S(2)}) collective-permute-start(bf16[32,64,1024]{2,1,0:T(8,128)(2,1)} %all-to-all-done.2.refs_0_.refs_1_.refs_2_.refs_3_), channel_id=1, source_target_pairs={{64,0},{65,1},{66,2},{67,3},{68,4},{69,5},{70,6},{71,7},{72,8},{73... | collective-permute-start | bytes 12582920 | tf_op jit(solution)/shard_map/ppermute | solution.py:592
  391.3 12.8 %assemble.1 = (f32[3,1024,512]{2,1,0:T(8,128)}, f32[512,1024]{1,0:T(8,128)}, f32[1024,1024]{1,0:T(8,128)}, f32[1024,1024]{1,0:T(8,128)}) custom-call(s32[2]{0:T(128)S(1)} %pad_add_fusion.core, bf16[32,64,1024]{2,1,0:T(8,128)(2,1)} %all-to-all-done.2.refs_0_.refs_1_.refs_2_.refs_3_, bf16[32,64,1024]{2,1,0:T(8,128)(2,1)} %all-to-all-done.2.refs_0_.refs_1_.refs_2_.refs_3_, ...), custom_call_target="tpu_custom_call" | custom-call | tf_op jit(solution)/shard_map/assemble/pallas_call | solution.py:376
  (170 shorter events, 56.6 us)
Async XLA Ops:
  7.2 8.0 %collective-permute-start.2 = (bf16[3,1024,512]{2,1,0:T(8,128)(2,1)}, bf16[3,1024,512]{2,1,0:T(8,128)(2,1)}, u32[]{:S(2)}, u32[]{:S(2)}) collective-permute-start(bf16[3,1024,512]{2,1,0:T(8,128)(2,1)} %bitcast.45), channel_id=1, source_target_pairs={{0,64},{64,0},{1,65},{65,1},{2,66},{66,2},{3,67},{67,3},{4,68},{68... | collective-permute-start | bytes 9437192 | tf_op jit(solution)/shard_map/ppermute | solution.py:496
  7.9 7.2 %collective-permute-start.3 = (bf16[512,1024]{1,0:T(8,128)(2,1)}, bf16[512,1024]{1,0:T(8,128)(2,1)S(1)}, u32[]{:S(2)}, u32[]{:S(2)}) collective-permute-start(bf16[512,1024]{1,0:T(8,128)(2,1)} %bitcast.48), channel_id=1, source_target_pairs={{0,64},{64,0},{1,65},{65,1},{2,66},{66,2},{3,67},{67,3},{4,68},{68... | collective-permute-start | bytes 3145736 | tf_op jit(solution)/shard_map/ppermute | solution.py:496
  8.0 7.0 %collective-permute-start = (bf16[128,1024]{1,0:T(8,128)(2,1)}, bf16[128,1024]{1,0:T(8,128)(2,1)S(1)}, u32[]{:S(2)}, u32[]{:S(2)}) collective-permute-start(bf16[128,1024]{1,0:T(8,128)(2,1)} %bitcast.4), channel_id=1, source_target_pairs={{0,32},{32,64},{1,33},{33,65},{2,34},{34,66},{3,35},{35,67},{4,36}... | collective-permute-start | bytes 786440 | tf_op jit(solution)/shard_map/ppermute | solution.py:484
  8.7 6.5 %collective-permute-start.1 = (bf16[128,1024]{1,0:T(8,128)(2,1)}, bf16[128,1024]{1,0:T(8,128)(2,1)S(1)}, u32[]{:S(2)}, u32[]{:S(2)}) collective-permute-start(bf16[128,1024]{1,0:T(8,128)(2,1)} %bitcast.4), channel_id=1, source_target_pairs={{32,96},{33,97},{34,98},{35,99},{36,100},{37,101},{38,102},{39,103... | collective-permute-start | bytes 786440 | tf_op jit(solution)/shard_map/ppermute | solution.py:485
  12.1 2.9 collective-permute-start.4
  15.9 27.8 %collective-permute-start.8 = (bf16[1024,1024]{1,0:T(8,128)(2,1)}, bf16[1024,1024]{1,0:T(8,128)(2,1)S(1)}, u32[]{:S(2)}, u32[]{:S(2)}) collective-permute-start(bf16[1024,1024]{1,0:T(8,128)(2,1)} %bitcast.46), channel_id=1, source_target_pairs={{0,64},{64,0},{1,65},{65,1},{2,66},{66,2},{3,67},{67,3},{4,68},{68... | collective-permute-start | bytes 6291464 | tf_op jit(solution)/shard_map/ppermute | solution.py:501
  20.2 25.1 %collective-permute-start.9 = (bf16[1024,1024]{1,0:T(8,128)(2,1)}, bf16[1024,1024]{1,0:T(8,128)(2,1)}, u32[]{:S(2)}, u32[]{:S(2)}) collective-permute-start(bf16[1024,1024]{1,0:T(8,128)(2,1)} %bitcast.47), channel_id=1, source_target_pairs={{0,64},{64,0},{1,65},{65,1},{2,66},{66,2},{3,67},{67,3},{4,68},{68... | collective-permute-start | bytes 6291464 | tf_op jit(solution)/shard_map/ppermute | solution.py:501
  24.2 38.8 %copy-start.6 = (bf16[512,1024]{1,0:T(8,128)(2,1)}, bf16[512,1024]{1,0:T(8,128)(2,1)S(1)}, u32[]{:S(2)}) copy-start(bf16[512,1024]{1,0:T(8,128)(2,1)S(1)} %get-tuple-element.171.out_w) | copy-start | bytes 3145732
  36.2 7.6 %collective-permute-start.5 = (bf16[128,1024]{1,0:T(8,128)(2,1)S(1)}, bf16[128,1024]{1,0:T(8,128)(2,1)S(1)}, u32[]{:S(2)}, u32[]{:S(2)}) collective-permute-start(bf16[128,1024]{1,0:T(8,128)(2,1)S(1)} %get-tuple-element.92), channel_id=1, source_target_pairs={{0,32},{32,0},{1,33},{33,1},{2,34},{34,2},{3,35},{35,3},{4,36},{36... | collective-permute-start | bytes 786440 | tf_op jit(solution)/shard_map/ppermute | solution.py:513
  54.8 8.1 %collective-permute-start.10 = (bf16[128,1024]{1,0:T(8,128)(2,1)S(1)}, bf16[128,1024]{1,0:T(8,128)(2,1)S(1)}, u32[]{:S(2)}, u32[]{:S(2)}) collective-permute-start(bf16[128,1024]{1,0:T(8,128)(2,1)S(1)} %get-tuple-element.100), channel_id=1, source_target_pairs={{0,32},{32,0},{1,33},{33,1},{2,34},{34,2},{3,35},{35,3},{4,36},{36... | collective-permute-start | bytes 786440 | tf_op jit(solution)/shard_map/ppermute | solution.py:513
  55.1 18.4 %collective-permute-start.6 = (bf16[128,1024]{1,0:T(8,128)(2,1)}, bf16[128,1024]{1,0:T(8,128)(2,1)}, u32[]{:S(2)}, u32[]{:S(2)}) collective-permute-start(bf16[128,1024]{1,0:T(8,128)(2,1)} %bitcast.4), channel_id=1, source_target_pairs={{64,32},{65,33},{66,34},{67,35},{68,36},{69,37},{70,38},{71,39},{7... | collective-permute-start | bytes 786440 | tf_op jit(solution)/shard_map/ppermute | solution.py:527
  56.5 17.0 %collective-permute-start.7 = (bf16[128,1024]{1,0:T(8,128)(2,1)}, bf16[128,1024]{1,0:T(8,128)(2,1)}, u32[]{:S(2)}, u32[]{:S(2)}) collective-permute-start(bf16[128,1024]{1,0:T(8,128)(2,1)} %bitcast.4), channel_id=1, source_target_pairs={{64,0},{96,64},{65,1},{97,65},{66,2},{98,66},{67,3},{99,67},{68,4}... | collective-permute-start | bytes 786440 | tf_op jit(solution)/shard_map/ppermute | solution.py:526
  62.9 16.7 %copy-start.3 = (bf16[1024,1024]{1,0:T(8,128)(2,1)S(1)}, bf16[1024,1024]{1,0:T(8,128)(2,1)}, u32[]{:S(2)}) copy-start(bf16[1024,1024]{1,0:T(8,128)(2,1)} %get-tuple-element.169.up_w) | copy-start | bytes 6291460
  73.5 5.4 %collective-permute-start.11 = (bf16[128,1024]{1,0:T(8,128)(2,1)}, bf16[128,1024]{1,0:T(8,128)(2,1)S(1)}, u32[]{:S(2)}, u32[]{:S(2)}) collective-permute-start(bf16[128,1024]{1,0:T(8,128)(2,1)} %get-tuple-element.103), channel_id=1, source_target_pairs={{0,32},{32,0},{1,33},{33,1},{2,34},{34,2},{3,35},{35,3},{4,36},{36... | collective-permute-start | bytes 786440 | tf_op jit(solution)/shard_map/ppermute | solution.py:513
  88.5 11.6 %collective-permute-start.13 = (bf16[128,3072]{1,0:T(8,128)(2,1)S(1)}, bf16[128,3072]{1,0:T(8,128)(2,1)S(1)}, u32[]{:S(2)}, u32[]{:S(2)}) collective-permute-start(bf16[128,3072]{1,0:T(8,128)(2,1)S(1)} %get-tuple-element.110), channel_id=1, source_target_pairs={{0,64},{64,0},{1,65},{65,1},{2,66},{66,2},{3,67},{67,3},{4,68},{68... | collective-permute-start | bytes 2359304 | tf_op jit(solution)/shard_map/ppermute | solution.py:516
  92.1 7.9 %collective-permute-start.14 = (bf16[128,1024]{1,0:T(8,128)(2,1)S(1)}, bf16[128,1024]{1,0:T(8,128)(2,1)S(1)}, u32[]{:S(2)}, u32[]{:S(2)}) collective-permute-start(bf16[128,1024]{1,0:T(8,128)(2,1)S(1)} %get-tuple-element.113), channel_id=1, source_target_pairs={{0,32},{32,0},{1,33},{33,1},{2,34},{34,2},{3,35},{35,3},{4,36},{36... | collective-permute-start | bytes 786440 | tf_op jit(solution)/shard_map/ppermute | solution.py:513
  92.1 13.5 %collective-permute-start.12 = (bf16[128,1024]{1,0:T(8,128)(2,1)S(1)}, bf16[128,1024]{1,0:T(8,128)(2,1)S(1)}, u32[]{:S(2)}, u32[]{:S(2)}) collective-permute-start(bf16[128,1024]{1,0:T(8,128)(2,1)S(1)} %get-tuple-element.108), channel_id=1, source_target_pairs={{0,32},{32,0},{1,33},{33,1},{2,34},{34,2},{3,35},{35,3},{4,36},{36... | collective-permute-start | bytes 786440 | tf_op jit(solution)/shard_map/ppermute | solution.py:513
  111.9 2.9 collective-permute-start.16
  112.9 7.9 %collective-permute-start.15 = (bf16[128,1024]{1,0:T(8,128)(2,1)S(1)}, bf16[128,1024]{1,0:T(8,128)(2,1)S(1)}, u32[]{:S(2)}, u32[]{:S(2)}) collective-permute-start(bf16[128,1024]{1,0:T(8,128)(2,1)S(1)} %get-tuple-element.121), channel_id=1, source_target_pairs={{0,32},{32,0},{1,33},{33,1},{2,34},{34,2},{3,35},{35,3},{4,36},{36... | collective-permute-start | bytes 786440 | tf_op jit(solution)/shard_map/ppermute | solution.py:513
  125.1 15.2 %copy-start.38 = (f32[8,1024]{1,0:T(8,128)}, f32[8,1024]{1,0:T(8,128)S(1)}, u32[]{:S(2)}) copy-start(f32[8,1024]{1,0:T(8,128)S(1)} %get-tuple-element.158) | copy-start | bytes 98308
  125.2 2.9 collective-permute-start.18
  126.1 7.9 %collective-permute-start.17 = (bf16[128,1024]{1,0:T(8,128)(2,1)S(1)}, bf16[128,1024]{1,0:T(8,128)(2,1)S(1)}, u32[]{:S(2)}, u32[]{:S(2)}) collective-permute-start(bf16[128,1024]{1,0:T(8,128)(2,1)S(1)} %get-tuple-element.132), channel_id=1, source_target_pairs={{0,32},{32,0},{1,33},{33,1},{2,34},{34,2},{3,35},{35,3},{4,36},{36... | collective-permute-start | bytes 786440 | tf_op jit(solution)/shard_map/ppermute | solution.py:513
  141.2 2.8 collective-permute-start.20
  142.0 7.9 %collective-permute-start.19 = (bf16[128,1024]{1,0:T(8,128)(2,1)S(1)}, bf16[128,1024]{1,0:T(8,128)(2,1)S(1)}, u32[]{:S(2)}, u32[]{:S(2)}) collective-permute-start(bf16[128,1024]{1,0:T(8,128)(2,1)S(1)} %get-tuple-element.142), channel_id=1, source_target_pairs={{0,32},{32,0},{1,33},{33,1},{2,34},{34,2},{3,35},{35,3},{4,36},{36... | collective-permute-start | bytes 786440 | tf_op jit(solution)/shard_map/ppermute | solution.py:513
  150.0 66.0 %all-to-all-start = ((bf16[32,64,1024]{2,1,0:T(8,128)(2,1)}), bf16[32,64,1024]{2,1,0:T(8,128)(2,1)}, u32[]{:S(2)}, u32[]{:S(2)}) async-start(bf16[32,64,1024]{2,1,0:T(8,128)(2,1)} %bitcast.37), calls=%async_computation | async-start | bytes 8388608 | tf_op jit(solution)/shard_map/all_to_all | solution.py:463
  159.0 218.7 %all-gather.3.cloned.1.call-start = ((), (), s32[]{:S(2)}) async-start(), calls=%async_computation.3 | async-start | bytes 4866048 | tf_op jit(solution)/shard_map/all_gather | solution.py:589
  159.6 59.5 %collective-permute-start.21 = (f32[128,1024]{1,0:T(8,128)S(1)}, f32[128,1024]{1,0:T(8,128)S(1)}, u32[]{:S(2)}, u32[]{:S(2)}) collective-permute-start(f32[128,1024]{1,0:T(8,128)S(1)} %broadcast_select_fusion.8), channel_id=1, source_target_pairs={{0,64},{96,32},{1,65},{97,33},{2,66},{98,34},{3,67},{99,35},{4,68}... | collective-permute-start | bytes 1572872 | tf_op jit(solution)/shard_map/ppermute | solution.py:586
  162.9 1.5 collective-permute-start.23
  164.5 41.4 %collective-permute-start.24 = (f32[6,1024]{1,0:T(8,128)S(1)}, f32[6,1024]{1,0:T(8,128)S(1)}, u32[]{:S(2)}, u32[]{:S(2)}) collective-permute-start(f32[6,1024]{1,0:T(8,128)S(1)} %slice.38), channel_id=1, source_target_pairs={{0,32},{32,0},{1,33},{33,1},{2,34},{34,2},{3,35},{35,3},{4,36},{36... | collective-permute-start | bytes 73736 | tf_op jit(solution)/shard_map/ppermute | solution.py:513
  285.5 93.4 %all-to-all-start.2 = ((bf16[32,64,1024]{2,1,0:T(8,128)(2,1)}), bf16[32,64,1024]{2,1,0:T(8,128)(2,1)}, u32[]{:S(2)}, u32[]{:S(2)}) async-start(bf16[32,64,1024]{2,1,0:T(8,128)(2,1)} %copy-done.4), calls=%async_computation.2 | async-start | bytes 8388608 | tf_op jit(solution)/shard_map/all_to_all | solution.py:463
  377.7 13.7 %collective-permute-start.25 = (bf16[32,72,1024]{2,1,0:T(8,128)(2,1)}, bf16[32,72,1024]{2,1,0:T(8,128)(2,1)}, u32[]{:S(2)}, u32[]{:S(2)}) collective-permute-start(bf16[32,72,1024]{2,1,0:T(8,128)(2,1)} %bitcast.39), channel_id=1, source_target_pairs={{0,64},{1,65},{2,66},{3,67},{4,68},{5,69},{6,70},{7,71},{8,72},{9,... | collective-permute-start | bytes 14155784 | tf_op jit(solution)/shard_map/ppermute | solution.py:591
  379.0 12.4 %collective-permute-start.22 = (bf16[32,64,1024]{2,1,0:T(8,128)(2,1)}, bf16[32,64,1024]{2,1,0:T(8,128)(2,1)}, u32[]{:S(2)}, u32[]{:S(2)}) collective-permute-start(bf16[32,64,1024]{2,1,0:T(8,128)(2,1)} %all-to-all-done.2.refs_0_.refs_1_.refs_2_.refs_3_), channel_id=1, source_target_pairs={{64,0},{65,1},{66,2},{67,3},{68,4},{69,5},{70,6},{71,7},{72,8},{73... | collective-permute-start | bytes 12582920 | tf_op jit(solution)/shard_map/ppermute | solution.py:592
  (46 other events, 215.4 us)
Sparse Core Ops, SparseCore 0:
  219.9 157.6 all-gather.2
